TPU v7x, 32 devices: a whole 2x2x4 slice. The times are simulated.
32 devices in a mesh: groups: 2 (over y), rows: 16 (over z, x, core).
Axes of the slice: x: 2, y: 2, z: 4, core: 2. Of those that a mesh axis runs over, the one named last changes fastest.
Arguments:
- latent: bfloat16 [64, 256, 512], P(('groups', 'rows')), parts along dimension 0, may hold values from -100 to 100
- gain_in: float32 [512], replicated, may hold values from 0.1 to 1.9
- shift_in: float32 [512], replicated, may hold values from -3 to 3
- conv_in: bfloat16 [4608, 256], replicated, may hold values from -0.09375 to 0.09375
- gain_mid: float32 [256], replicated, may hold values from 0.1 to 1.9
- shift_mid: float32 [256], replicated, may hold values from -3 to 3
- conv_mid: bfloat16 [2304, 256], replicated, may hold values from -0.125 to 0.125
- skip_weight: bfloat16 [512, 256], replicated, may hold values from -0.25 to 0.25
Outputs:
- decoded: bfloat16 [128, 512, 256], P(('groups', 'rows')), parts along dimension 0
There are 2 independent parts, one for each index of `groups`. A program takes and returns all parts, laid end to end along the dimension named above; an argument that names none is the same for every part. Nothing has to cross between parts.
All inputs are finite; a program needn't handle non-finite values.
Results may differ from a plain program's by a relative error of at most 0.009.
Values may be sent and summed in bfloat16 or wider, within the bound.
No kernel may reach another device: no remote copies, remote signals or barrier semaphores. Data moves between devices by JAX's collectives and lax.ppermute only.
A program may use at most 64 MiB of HBM per device.

v0:
```python
import jax
import jax.numpy as jnp
from jax import lax
from jax.sharding import PartitionSpec as P

GROUPS = 32


def padded_2(cells, sides, width):
    for axis, dim in sides:
        count = lax.axis_size(axis)
        ends = count - 1
        head = lax.slice_in_dim(cells, 0, width, axis=dim)
        tail = lax.slice_in_dim(cells, cells.shape[dim] - width, cells.shape[dim], axis=dim)
        cells = jnp.concatenate(
            [
                lax.ppermute(tail, axis, [(i, (i + 1) % count) for i in range(ends)]),
                cells,
                lax.ppermute(head, axis, [((i + 1) % count, i) for i in range(ends)]),
            ],
            axis=dim,
        )
    return cells


def upsample(values):
    return jnp.repeat(jnp.repeat(values, 2, axis=0), 2, axis=1)


def pad_columns(values):
    return jnp.pad(values, ((0, 0), (1, 1), (0, 0)))


def normalize(values, gain, shift):
    height, breadth, chans = values.shape
    width_group = chans // GROUPS
    grouped = values.reshape(height * breadth, GROUPS, width_group)
    count = float(height * breadth * width_group * lax.axis_size("rows"))
    summed, squared = lax.psum(
        (jnp.sum(grouped, axis=(0, 2)), jnp.sum(grouped * grouped, axis=(0, 2))), "rows"
    )
    center = summed / count
    spread = squared / count - center * center
    deviate = grouped - center[None, :, None]
    normed = deviate / jnp.sqrt(spread[None, :, None] + 1e-06)
    return jax.nn.silu(normed.reshape(height, breadth, chans) * gain + shift)


def convolve(padded, weight):
    height = padded.shape[0] - 2
    breadth = padded.shape[1] - 2
    chans = padded.shape[2]
    accum = jnp.zeros((height * breadth, weight.shape[1]), jnp.float32)
    for offset_index in range(9):
        shift_row = offset_index // 3
        shift_col = offset_index % 3
        window = padded[shift_row : shift_row + height, shift_col : shift_col + breadth].reshape(
            -1, chans
        )
        accum = accum + jnp.dot(
            window,
            weight[offset_index * chans : (offset_index + 1) * chans],
            preferred_element_type=jnp.float32,
        )
    return accum.reshape(height, breadth, -1)


def body(latent, gain_in, shift_in, conv_in, gain_mid, shift_mid, conv_mid, skip_weight):
    act = normalize(latent.astype(jnp.float32), gain_in, shift_in).astype(jnp.bfloat16)
    tall = padded_2(upsample(act), (("rows", 0),), 1)
    padded = pad_columns(tall)
    upsampled = tall[1:-1]
    out_rows, out_cols, in_chans = upsampled.shape
    flat_up = upsampled.reshape(-1, in_chans)
    hidden = convolve(padded, conv_in).astype(jnp.bfloat16)
    middle = normalize(hidden.astype(jnp.float32), gain_mid, shift_mid).astype(jnp.bfloat16)
    mid_padded = pad_columns(padded_2(middle, (("rows", 0),), 1))
    second = convolve(mid_padded, conv_mid)
    skipped = jnp.dot(flat_up, skip_weight, preferred_element_type=jnp.float32)
    total_out = second + skipped.reshape(out_rows, out_cols, -1)
    return total_out.astype(jnp.bfloat16)


def solution(mesh):
    placed = (P(("groups", "rows"), None, None), P(), P(), P(), P(), P(), P(), P())
    return jax.shard_map(
        body,
        mesh=mesh,
        in_specs=placed,
        out_specs=P(("groups", "rows"), None, None),
        check_vma=False,
    )
```

profile of v0, /device:TPU:1, one launch (start us, length us, event | category | flops | bytes accessed | tf_op | source)
XLA Modules:
  0.0 117.0 jit_solution(15183971117016011453)
XLA Ops:
  0.0 1.3 %convert_reduce_fusion = (f32[512]{0:T(512)S(1)}, f32[512]{0:T(512)S(1)}) fusion(bf16[2,256,512]{2,1,0:T(8,128)(2,1)} %param.8), kind=kLoop, calls=%fused_computation.38 | loop fusion | flops 1047552 | bytes 528384 | tf_op jit(solution)/shard_map/reduce_sum | solution.py:40
  1.7 30.5 %all-reduce.3 = (f32[32]{0:T(128)S(1)}, f32[32]{0:T(128)S(1)}) all-reduce(f32[32]{0:T(128)S(1)} %reduce_sum.54, f32[32]{0:T(128)S(1)} %reduce_sum.51), channel_id=1, replica_groups=mesh['groups'=2,'rows'=16] {'rows'}, use_global_device_ids=true, to_apply=%region_5.6 | all-reduce | flops 64 | bytes 512 | tf_op jit(solution)/shard_map/psum | solution.py:39
  32.5 1.4 %multiply_convert_fusion.3 = bf16[2,256,512]{2,1,0:T(8,128)(2,1)S(1)} fusion(bf16[2,256,512]{2,1,0:T(8,128)(2,1)} %param.8, f32[512]{0:T(512)} %param.10, f32[512]{0:T(512)} %param.9, f32[512]{0:T(512)S(1)} %div.57, f32[512]{0:T(512)S(1)} %sub.38), kind=kLoop, calls=%fused_computation.50 | loop fusion | flops 2621440 | bytes 1056768 | tf_op jit(solution)/shard_map/convert_element_type | solution.py:69
  34.4 1.0 broadcast_in_dim.24
  35.4 3.0 %collective-permute-start = (bf16[1,512,512]{2,1,0:T(8,128)(2,1)}, bf16[1,512,512]{2,1,0:T(8,128)(2,1)S(1)}, u32[]{:S(2)}, u32[]{:S(2)}) collective-permute-start(bf16[1,512,512]{2,1,0:T(8,128)(2,1)} %broadcast_in_dim.24), channel_id=1, source_target_pairs={{0,1},{1,2},{2,3},{3,4},{4,5},{5,6},{6,7},{7,8},{8,9},{9,10},{10,1... | collective-permute-start | bytes 1572872 | tf_op jit(solution)/shard_map/ppermute | solution.py:17
  38.6 1.0 broadcast_in_dim.27
  39.6 4.6 %collective-permute-start.1 = (bf16[1,512,512]{2,1,0:T(8,128)(2,1)}, bf16[1,512,512]{2,1,0:T(8,128)(2,1)S(1)}, u32[]{:S(2)}, u32[]{:S(2)}) collective-permute-start(bf16[1,512,512]{2,1,0:T(8,128)(2,1)} %broadcast_in_dim.27), channel_id=1, source_target_pairs={{1,0},{2,1},{3,2},{4,3},{5,4},{6,5},{7,6},{8,7},{9,8},{10,9},{11,1... | collective-permute-start | bytes 1572872 | tf_op jit(solution)/shard_map/ppermute | solution.py:19
  44.3 2.4 %broadcast_in_dim.25 = bf16[4,256,2,512]{3,2,1,0:T(2,128)(2,1)} broadcast(bf16[4,256,512]{2,1,0:T(8,128)(2,1)S(1)} %bitcast.55), dimensions={0,1,3} | broadcast | bytes 3145728 | tf_op jit(solution)/shard_map/broadcast_in_dim | solution.py:27
  46.7 2.7 %reshape.106 = bf16[4,512,512]{2,1,0:T(8,128)(2,1)S(1)} reshape(bf16[4,256,2,512]{3,2,1,0:T(2,128)(2,1)} %broadcast_in_dim.25) | data formatting | bytes 4194304 | tf_op jit(solution)/shard_map/reshape | solution.py:27
  49.4 4.1 %reshape.111 = bf16[2048,512]{1,0:T(8,128)(2,1)} reshape(bf16[4,256,2,512]{3,2,1,0:T(2,128)(2,1)} %broadcast_in_dim.25) | data formatting | bytes 4194304 | tf_op jit(solution)/shard_map/reshape | solution.py:57
  53.6 2.3 %fusion.36 = f32[2048,256]{1,0:T(8,128)S(1)} fusion(bf16[2048,512]{1,0:T(8,128)(2,1)} %reshape.111, bf16[4608,256]{1,0:T(8,128)(2,1)} %param.11), kind=kOutput, calls=%fused_computation.62 | convolution fusion | flops 536870912 | bytes 4456448 | tf_op jit(solution)/shard_map/dot_general | solution.py:60
  55.9 1.0 fusion.5
  56.9 2.0 %fusion.59 = (bf16[4,512,512]{2,1,0:T(8,128)(2,1)S(1)}, bf16[4,512,512]{2,1,0:T(8,128)(2,1)S(1)}, bf16[4,512,512]{2,1,0:T(8,128)(2,1)S(1)}, bf16[4,512,512]{2,1,...) fusion(bf16[6,514,512]{2,1,0:T(8,128)(2,1)S(1)} %fusion.5), kind=kLoop, calls=%fused_computation.89 | loop fusion | bytes 25165824 | tf_op jit(solution)/shard_map/slice | solution.py:57
  64.4 2.8 %fusion.58 = (f32[256]{0:T(256)S(1)}, f32[256]{0:T(256)S(1)}, f32[2048,256]{1,0:T(8,128)}) fusion(f32[2048,256]{1,0:T(8,128)S(1)} %fusion.29, f32[2048,256]{1,0:T(8,128)S(1)} %fusion.31, f32[2048,256]{1,0:T(8,128)S(1)} %fusion.33, bf16[2048,512]{1,0:T(8,128)(2,1)S(1)} %bitcast.52, bf16[4608,256]{1,0:T(8,128)(2,1)S(1)} %copy-done.2, ...), kind=kOutput, calls=%fused_computation.88 | convolution fusion | flops 543686144 | bytes 21235712 | tf_op jit(solution)/shard_map/dot_general | solution.py:60
  67.5 28.2 %all-reduce.2 = (f32[32]{0:T(128)S(1)}, f32[32]{0:T(128)S(1)}) all-reduce(f32[32]{0:T(128)S(1)} %reduce_sum.75, f32[32]{0:T(128)S(1)} %reduce_sum.72), channel_id=1, replica_groups=mesh['groups'=2,'rows'=16] {'rows'}, use_global_device_ids=true, to_apply=%region_11.12 | all-reduce | flops 64 | bytes 512 | tf_op jit(solution)/shard_map/psum | solution.py:39
  96.1 2.3 %multiply_convert_fusion.1 = bf16[4,512,256]{2,1,0:T(8,128)(2,1)S(1)} fusion(f32[4,512,256]{2,1,0:T(8,128)} %bitcast.53, f32[256]{0:T(256)S(1)} %copy-done.4, f32[256]{0:T(256)S(1)} %copy-done.5, f32[256]{0:T(256)S(1)} %div.64, f32[256]{0:T(256)S(1)} %sub.43), kind=kLoop, calls=%fused_computation.29 | loop fusion | flops 4718592 | bytes 3149824 | tf_op jit(solution)/shard_map/convert_element_type | solution.py:76
  98.4 1.9 %collective-permute-start.2 = (bf16[1,512,256]{2,1,0:T(8,128)(2,1)S(1)}, bf16[1,512,256]{2,1,0:T(8,128)(2,1)S(1)}, u32[]{:S(2)}, u32[]{:S(2)}) collective-permute-start(bf16[1,512,256]{2,1,0:T(8,128)(2,1)S(1)} %get-tuple-element.29), channel_id=1, source_target_pairs={{0,1},{1,2},{2,3},{3,4},{4,5},{5,6},{6,7},{7,8},{8,9},{9,10},{10,1... | collective-permute-start | bytes 786440 | tf_op jit(solution)/shard_map/ppermute | solution.py:17
  100.4 3.3 %collective-permute-start.3 = (bf16[1,512,256]{2,1,0:T(8,128)(2,1)S(1)}, bf16[1,512,256]{2,1,0:T(8,128)(2,1)S(1)}, u32[]{:S(2)}, u32[]{:S(2)}) collective-permute-start(bf16[1,512,256]{2,1,0:T(8,128)(2,1)S(1)} %get-tuple-element.30), channel_id=1, source_target_pairs={{1,0},{2,1},{3,2},{4,3},{5,4},{6,5},{7,6},{8,7},{9,8},{10,9},{11,1... | collective-permute-start | bytes 786440 | tf_op jit(solution)/shard_map/ppermute | solution.py:19
  104.4 2.1 %collective-permute-done.2 = bf16[1,512,256]{2,1,0:T(8,128)(2,1)S(1)} collective-permute-done((bf16[1,512,256]{2,1,0:T(8,128)(2,1)S(1)}, bf16[1,512,256]{2,1,0:T(8,128)(2,1)S(1)}, u32[]{:S(2)}, u32[]{:S(2)}) %collective-permute-start.2) | collective-permute-done | bytes 262176 | tf_op jit(solution)/shard_map/ppermute | solution.py:17
  106.5 1.6 %collective-permute-done.3 = bf16[1,512,256]{2,1,0:T(8,128)(2,1)S(1)} collective-permute-done((bf16[1,512,256]{2,1,0:T(8,128)(2,1)S(1)}, bf16[1,512,256]{2,1,0:T(8,128)(2,1)S(1)}, u32[]{:S(2)}, u32[]{:S(2)}) %collective-permute-start.3) | collective-permute-done | bytes 262176 | tf_op jit(solution)/shard_map/ppermute | solution.py:19
  108.5 0.8 fusion.60
  111.7 1.1 copy-done.1
  112.8 0.9 convolution_add_fusion.4
  115.7 1.3 %add_convert_fusion = bf16[4,512,256]{2,1,0:T(8,128)(2,1)} fusion(f32[4,512,256]{2,1,0:T(8,128)S(1)} %bitcast.51, f32[4,512,256]{2,1,0:T(8,128)S(1)} %fusion.27), kind=kLoop, calls=%fused_computation.27 | loop fusion | flops 1048576 | bytes 5242880 | tf_op jit(solution)/shard_map/convert_element_type | solution.py:81
  (55 shorter events, 12.9 us)
Async XLA Ops:
  0.0 103.7 %copy-start = (bf16[512,256]{1,0:T(8,128)(2,1)S(1)}, bf16[512,256]{1,0:T(8,128)(2,1)}, u32[]{:S(2)}) copy-start(bf16[512,256]{1,0:T(8,128)(2,1)} %param.15) | copy-start | bytes 786436
  35.4 20.5 %collective-permute-start = (bf16[1,512,512]{2,1,0:T(8,128)(2,1)}, bf16[1,512,512]{2,1,0:T(8,128)(2,1)S(1)}, u32[]{:S(2)}, u32[]{:S(2)}) collective-permute-start(bf16[1,512,512]{2,1,0:T(8,128)(2,1)} %broadcast_in_dim.24), channel_id=1, source_target_pairs={{0,1},{1,2},{2,3},{3,4},{4,5},{5,6},{6,7},{7,8},{8,9},{9,10},{10,1... | collective-permute-start | bytes 1572872 | tf_op jit(solution)/shard_map/ppermute | solution.py:17
  39.6 16.3 %collective-permute-start.1 = (bf16[1,512,512]{2,1,0:T(8,128)(2,1)}, bf16[1,512,512]{2,1,0:T(8,128)(2,1)S(1)}, u32[]{:S(2)}, u32[]{:S(2)}) collective-permute-start(bf16[1,512,512]{2,1,0:T(8,128)(2,1)} %broadcast_in_dim.27), channel_id=1, source_target_pairs={{1,0},{2,1},{3,2},{4,3},{5,4},{6,5},{7,6},{8,7},{9,8},{10,9},{11,1... | collective-permute-start | bytes 1572872 | tf_op jit(solution)/shard_map/ppermute | solution.py:19
  56.9 2.0 %copy-start.2 = (bf16[4608,256]{1,0:T(8,128)(2,1)S(1)}, bf16[4608,256]{1,0:T(8,128)(2,1)}, u32[]{:S(2)}) copy-start(bf16[4608,256]{1,0:T(8,128)(2,1)} %param.11) | copy-start | bytes 7077892
  64.4 31.8 %copy-start.4 = (f32[256]{0:T(256)S(1)}, f32[256]{0:T(256)}, u32[]{:S(2)}) copy-start(f32[256]{0:T(256)} %param.13) | copy-start | bytes 3076
  64.4 31.8 %copy-start.5 = (f32[256]{0:T(256)S(1)}, f32[256]{0:T(256)}, u32[]{:S(2)}) copy-start(f32[256]{0:T(256)} %param.12) | copy-start | bytes 3076
  98.4 8.0 %collective-permute-start.2 = (bf16[1,512,256]{2,1,0:T(8,128)(2,1)S(1)}, bf16[1,512,256]{2,1,0:T(8,128)(2,1)S(1)}, u32[]{:S(2)}, u32[]{:S(2)}) collective-permute-start(bf16[1,512,256]{2,1,0:T(8,128)(2,1)S(1)} %get-tuple-element.29), channel_id=1, source_target_pairs={{0,1},{1,2},{2,3},{3,4},{4,5},{5,6},{6,7},{7,8},{8,9},{9,10},{10,1... | collective-permute-start | bytes 786440 | tf_op jit(solution)/shard_map/ppermute | solution.py:17
  100.4 7.7 %collective-permute-start.3 = (bf16[1,512,256]{2,1,0:T(8,128)(2,1)S(1)}, bf16[1,512,256]{2,1,0:T(8,128)(2,1)S(1)}, u32[]{:S(2)}, u32[]{:S(2)}) collective-permute-start(bf16[1,512,256]{2,1,0:T(8,128)(2,1)S(1)} %get-tuple-element.30), channel_id=1, source_target_pairs={{1,0},{2,1},{3,2},{4,3},{5,4},{6,5},{7,6},{8,7},{9,8},{10,9},{11,1... | collective-permute-start | bytes 786440 | tf_op jit(solution)/shard_map/ppermute | solution.py:19
  108.5 1.3 %copy-start.3 = (bf16[2304,256]{1,0:T(8,128)(2,1)S(1)}, bf16[2304,256]{1,0:T(8,128)(2,1)}, u32[]{:S(2)}) copy-start(bf16[2304,256]{1,0:T(8,128)(2,1)} %param.14) | copy-start | bytes 3538948
  111.2 1.6 %copy-start.1 = (f32[2048,256]{1,0:T(8,128)S(1)}, f32[2048,256]{1,0:T(8,128)}, u32[]{:S(2)}) copy-start(f32[2048,256]{1,0:T(8,128)} %get-tuple-element.37) | copy-start | bytes 6291460
where the time goes:
time: 117 us
  blocking collectives  58.8 us (50%)
  local copies, waits for them, and re-layouts  17.4 us (15%)
  matrix products  15.3 us (13%)
  starting transfers between devices  12.8 us (11%)
  other arithmetic  8.68 us (7%)
  waiting for transfers between devices  3.64 us (3%)
    psum x2, blocking collectives, normalize(): lax.psum((jnp.sum(grouped, axis=(0, 2)), jnp.sum(grouped * grouped, axis=...  58.8 us
    dot_general x18, matrix products, convolve(): jnp.dot(window, weight[offset_index * chans:(offset_index + 1) * chans],...  14.6 us
    ppermute x2, starting transfers between devices, padded_2(): lax.ppermute(head, axis, [((i + 1) % count, i) for i in range(ends)])  7.96 us
    broadcast_in_dim x6, local copies, waits for them, and re-layouts, upsample(): return jnp.repeat(jnp.repeat(values, 2, axis=0), 2, axis=1)  5.04 us
    ppermute x2, starting transfers between devices, padded_2(): lax.ppermute(tail, axis, [(i, (i + 1) % count) for i in range(ends)])  4.89 us
    reshape x1, local copies, waits for them, and re-layouts, convolve(): padded[shift_row:shift_row + height, shift_col:shift_col + breadth]  4.13 us
    slice x2, local copies, waits for them, and re-layouts, convolve(): padded[shift_row:shift_row + height, shift_col:shift_col + breadth]  2.84 us
    reshape x1, local copies, waits for them, and re-layouts, upsample(): return jnp.repeat(jnp.repeat(values, 2, axis=0), 2, axis=1)  2.75 us
  transfers between devices with their start and end apart: 4, of which 2 were waited for; matrix products, arithmetic and copies ran while one was open for 12% of the time, Pallas kernels for 0%

commit v1 on v0

v1 whole, which is shorter than its diff:
```python
import functools

import jax
import jax.numpy as jnp
from jax import lax
from jax.experimental import pallas as pl
from jax.experimental.pallas import tpu as pltpu
from jax.sharding import PartitionSpec as P

GROUPS = 32
EPS = 1e-06
F32 = jnp.float32
BF16 = jnp.bfloat16
LANES = 128
VMEM = pltpu.VMEM


def vmem_spec():
    return pl.BlockSpec(memory_space=VMEM)


def params(limit_mib):
    return pltpu.CompilerParams(vmem_limit_bytes=limit_mib << 20)


def cost(flops, data):
    return pl.CostEstimate(flops=flops, bytes_accessed=data, transcendentals=0)


def stack_lanes(row):
    count = row.shape[1] // LANES
    return [row[:, i * LANES : (i + 1) * LANES] for i in range(count)]


def put_stats(out_ref, total, square):
    rows = stack_lanes(total) + stack_lanes(square)
    fill = 8 - len(rows)
    if fill:
        rows.append(jnp.zeros((fill, LANES), F32))
    tile = jnp.concatenate(rows, axis=0)
    out_ref[...] = jnp.broadcast_to(tile[None], out_ref.shape)


def get_affine(stats_ref, gain, shift, group_width, count):
    chans = gain.shape[1]
    half = chans // LANES
    total = jnp.sum(stats_ref[...], axis=0)
    left = lax.broadcasted_iota(jnp.int32, (LANES, LANES), 0) // group_width
    right = lax.broadcasted_iota(jnp.int32, (LANES, LANES), 1) // group_width
    same = (left == right).astype(F32)
    pooled = jnp.dot(total, same, preferred_element_type=F32, precision=lax.Precision.HIGHEST)
    scaled = pooled * (1.0 / count)
    center = jnp.concatenate([scaled[i : i + 1] for i in range(half)], axis=1)
    moment = jnp.concatenate([scaled[half + i : half + i + 1] for i in range(half)], axis=1)
    spread = jnp.maximum(moment - center * center, 0.0)
    scale = gain * lax.rsqrt(spread + EPS)
    return 0.5 * scale, 0.5 * (shift - center * scale)


def half_silu(values, scale, offset):
    halved = values * scale + offset
    return halved + halved * jnp.tanh(halved)


def shift_rows(values, step):
    size = values.shape[0]
    moved = pltpu.roll(values, step % size, 0)
    place = lax.broadcasted_iota(jnp.int32, (size, 1), 0)
    edge = 0 if step == 1 else size - 1
    return jnp.where(place == edge, 0.0, moved)


def stats_kernel(latent_ref, out_ref):
    values = latent_ref[...].astype(F32)
    values = values.reshape(-1, values.shape[-1])
    put_stats(
        out_ref,
        jnp.sum(values, axis=0, keepdims=True),
        jnp.sum(values * values, axis=0, keepdims=True),
    )


def combine_kernel(weight_ref, out_ref):
    chans = out_ref.shape[1] // 4
    step = 16

    def pairs(taps):
        return (taps[0], taps[1] + taps[2]), (taps[0] + taps[1], taps[2])

    @pl.loop(0, chans // step)
    def _(index):
        start = pl.multiple_of(index * step, step)
        taps = [
            [weight_ref[pl.ds((3 * a + b) * chans + start, step), :].astype(F32) for b in range(3)]
            for a in range(3)
        ]
        columns = [pairs([taps[a][b] for a in range(3)]) for b in range(3)]
        for row_phase in range(2):
            for row_tap in range(2):
                across = pairs([columns[b][row_phase][row_tap] for b in range(3)])
                for col_phase in range(2):
                    for col_tap in range(2):
                        out_ref[
                            2 * row_phase + col_phase,
                            pl.ds((2 * row_tap + col_tap) * chans + start, step),
                            :,
                        ] = across[col_phase][col_tap].astype(BF16)


def first_conv(act_ref, weights_ref, row_phase, col_phase, first, count):
    wide = act_ref.shape[2] // 3
    window = pl.ds(col_phase * wide, 2 * wide)
    lhs = jnp.concatenate(
        [
            act_ref[first + tap : first + tap + count, :, window].reshape(-1, 2 * wide)
            for tap in range(2)
        ],
        axis=1,
    )
    return jnp.dot(lhs, weights_ref[2 * row_phase + col_phase], preferred_element_type=F32)


def hidden_kernel(
    count,
    axis_count,
    stats_ref,
    up_ref,
    latent_ref,
    down_ref,
    gain_ref,
    shift_ref,
    weights_ref,
    act_ref,
    hidden_ref,
    out_ref,
):
    rows, cols, chans = latent_ref.shape
    scale, offset = get_affine(stats_ref, gain_ref[...], shift_ref[...], chans // GROUPS, count)
    place = lax.axis_index("rows")
    for row in range(rows + 2):
        if row == 0:
            source, keep = up_ref[0], place > 0
        elif row == rows + 1:
            source, keep = down_ref[0], place < axis_count - 1
        else:
            source, keep = latent_ref[row - 1], None
        act = half_silu(source.astype(F32), scale, offset)
        if keep is not None:
            act = act * keep.astype(F32)
        act_ref[row, :, 0:chans] = shift_rows(act, 1).astype(BF16)
        act_ref[row, :, chans : 2 * chans] = act.astype(BF16)
        act_ref[row, :, 2 * chans :] = shift_rows(act, -1).astype(BF16)
    totals, squares = [], []
    for row_phase in range(2):
        for col_phase in range(2):
            found = first_conv(act_ref, weights_ref, row_phase, col_phase, row_phase, rows)
            found = found.astype(BF16)
            for row in range(rows):
                hidden_ref[2 * row + row_phase, col_phase] = found[row * cols : (row + 1) * cols]
            wide = found.astype(F32)
            totals.append(jnp.sum(wide, axis=0, keepdims=True))
            squares.append(jnp.sum(wide * wide, axis=0, keepdims=True))
    put_stats(out_ref, sum(totals[1:], totals[0]), sum(squares[1:], squares[0]))


def border_kernel(act_ref, weights_ref, skip_ref, border_ref, skipped_ref):
    rows = act_ref.shape[0] - 2
    wide = act_ref.shape[2] // 3
    for col_phase in range(2):
        border_ref[0, col_phase] = first_conv(act_ref, weights_ref, 1, col_phase, 0, 1).astype(BF16)
        border_ref[1, col_phase] = first_conv(act_ref, weights_ref, 0, col_phase, rows, 1).astype(
            BF16
        )
    middle = act_ref[1 : 1 + rows, :, wide : 2 * wide].reshape(-1, wide)
    skipped_ref[...] = jnp.dot(middle, skip_ref[...], preferred_element_type=F32)


def output_kernel(
    count,
    axis_count,
    stats_ref,
    border_ref,
    hidden_ref,
    gain_ref,
    shift_ref,
    weight_ref,
    skipped_ref,
    out_ref,
    mid_ref,
    mixed_ref,
):
    rows, _, cols, chans = hidden_ref.shape
    scale, offset = get_affine(stats_ref, gain_ref[...], shift_ref[...], chans // GROUPS, count)
    place = lax.axis_index("rows")
    for row in range(rows + 2):
        pair = []
        for phase in range(2):
            if row == 0:
                source, keep = border_ref[0, phase], place > 0
            elif row == rows + 1:
                source, keep = border_ref[1, phase], place < axis_count - 1
            else:
                source, keep = hidden_ref[row - 1, phase], None
            value = half_silu(source.astype(F32), scale, offset)
            if keep is not None:
                value = value * keep.astype(F32)
            pair.append(value)
        even, odd = pair
        mid_ref[row, :, 0:chans] = shift_rows(odd, 1).astype(BF16)
        mid_ref[row, :, chans : 2 * chans] = even.astype(BF16)
        mid_ref[row, :, 2 * chans : 3 * chans] = odd.astype(BF16)
        mid_ref[row, :, 3 * chans :] = shift_rows(even, -1).astype(BF16)
    for row in range(rows):
        base = skipped_ref[pl.ds((row // 2) * cols, cols), :]
        for phase in range(2):
            lhs = jnp.concatenate(
                [mid_ref[row + tap, :, phase * chans : (phase + 3) * chans] for tap in range(3)],
                axis=1,
            )
            found = base + jnp.dot(lhs, weight_ref[...], preferred_element_type=F32)
            for part in range(chans // LANES):
                mixed_ref[part, pl.ds(phase, cols, stride=2), :] = found[
                    :, part * LANES : (part + 1) * LANES
                ]
        for part in range(chans // LANES):
            out_ref[row, :, part * LANES : (part + 1) * LANES] = mixed_ref[part].astype(BF16)


def body(latent, gain_in, shift_in, conv_in, gain_mid, shift_mid, conv_mid, skip_weight):
    axis = "rows"
    peers = lax.axis_size(axis)
    rows, cols, chans = latent.shape
    outs = conv_in.shape[1]
    ends = peers - 1
    up = lax.ppermute(latent[rows - 1 :], axis, [(i, i + 1) for i in range(ends)])
    down = lax.ppermute(latent[:1], axis, [(i + 1, i) for i in range(ends)])

    stats = pl.pallas_call(
        stats_kernel,
        out_shape=jax.ShapeDtypeStruct((peers, 8, LANES), F32),
        in_specs=[vmem_spec()],
        out_specs=vmem_spec(),
        compiler_params=params(16),
        name="stats",
    )(latent)
    stats = lax.all_to_all(stats, axis, 0, 0)

    weights = pl.pallas_call(
        combine_kernel,
        out_shape=jax.ShapeDtypeStruct((4, 4 * chans, outs), BF16),
        in_specs=[vmem_spec()],
        out_specs=vmem_spec(),
        compiler_params=params(16),
        cost_estimate=cost(4 << 20, 8 << 20),
        name="combine",
    )(conv_in)

    act, hidden, stats_mid = pl.pallas_call(
        functools.partial(
            hidden_kernel, float(rows * cols * (chans // GROUPS) * peers), peers
        ),
        out_shape=(
            jax.ShapeDtypeStruct((rows + 2, cols, 3 * chans), BF16),
            jax.ShapeDtypeStruct((2 * rows, 2, cols, outs), BF16),
            jax.ShapeDtypeStruct((peers, 8, LANES), F32),
        ),
        in_specs=[vmem_spec()] * 7,
        out_specs=(vmem_spec(),) * 3,
        compiler_params=params(24),
        name="hidden",
    )(stats, up, latent, down, gain_in.reshape(1, -1), shift_in.reshape(1, -1), weights)
    stats_mid = lax.all_to_all(stats_mid, axis, 0, 0)

    border, skipped = pl.pallas_call(
        border_kernel,
        out_shape=(
            jax.ShapeDtypeStruct((2, 2, cols, outs), BF16),
            jax.ShapeDtypeStruct((rows * cols, outs), F32),
        ),
        in_specs=[vmem_spec()] * 3,
        out_specs=(vmem_spec(),) * 2,
        compiler_params=params(24),
        cost_estimate=cost(1200 << 20, 8 << 20),
        name="border",
    )(act, weights, skip_weight)

    return pl.pallas_call(
        functools.partial(
            output_kernel, float(4 * rows * cols * (outs // GROUPS) * peers), peers
        ),
        out_shape=jax.ShapeDtypeStruct((2 * rows, 2 * cols, outs), BF16),
        in_specs=[vmem_spec()] * 7,
        out_specs=vmem_spec(),
        scratch_shapes=[
            VMEM((2 * rows + 2, cols, 4 * outs), BF16),
            VMEM((outs // LANES, 2 * cols, LANES), F32),
        ],
        compiler_params=params(24),
        name="output",
    )(
        stats_mid,
        border,
        hidden,
        gain_mid.reshape(1, -1),
        shift_mid.reshape(1, -1),
        conv_mid,
        skipped,
    )


def solution(mesh):
    placed = (P(("groups", "rows"), None, None), P(), P(), P(), P(), P(), P(), P())
    return jax.shard_map(
        body,
        mesh=mesh,
        in_specs=placed,
        out_specs=P(("groups", "rows"), None, None),
        check_vma=False,
    )
```

time: 117 us -> 44.3 us (0.38)
  the two profiles are of different devices: /device:TPU:1 before, /device:TPU:0 now
where the time goes in v1:
time: 44.3 us; the launch traced here: 43.8 us
  starting transfers between devices  15.8 us (36%)
  local copies, waits for them, and re-layouts  14.6 us (33%)
  Pallas kernels  10.3 us (23%)
  waiting for transfers between devices  2.99 us (7%)
    unnamed x28, local copies, waits for them, and re-layouts  13.5 us
    all_to_all x1, starting transfers between devices, body(): stats = lax.all_to_all(stats, axis, 0, 0)  7.94 us
    pallas_call x1, Pallas kernels, body(): pl.pallas_call(functools.partial(output_kernel, float(4 * rows * cols * (...  4.01 us
    all_to_all x1, starting transfers between devices, body(): stats_mid = lax.all_to_all(stats_mid, axis, 0, 0)  3.5 us
    pallas_call x1, Pallas kernels, body(): pl.pallas_call(functools.partial(hidden_kernel, float(rows * cols * (chan...  3.43 us
    ppermute x1, starting transfers between devices, body(): lax.ppermute(latent[rows - 1:], axis, [(i, i + 1) for i in range(ends)])  3.05 us
    all_to_all x1, waiting for transfers between devices, body(): stats = lax.all_to_all(stats, axis, 0, 0)  2.54 us
    pallas_call x1, Pallas kernels, body(): pl.pallas_call(border_kernel, out_shape=(jax.ShapeDtypeStruct((2, 2, cols...  1.38 us
  transfers between devices with their start and end apart: 4, of which 2 were waited for; matrix products, arithmetic and copies ran while one was open for 0% of the time, Pallas kernels for 6%

profile of v1, /device:TPU:0, one launch (start us, length us, event | category | flops | bytes accessed | tf_op | source)
XLA Modules:
  0.0 43.8 jit_solution(14968162066822653423)
XLA Ops:
  0.0 1.1 %fusion = (bf16[1,256,512]{2,1,0:T(8,128)(2,1)S(1)}, bf16[1,256,512]{2,1,0:T(8,128)(2,1)S(1)}) fusion(bf16[2,256,512]{2,1,0:T(8,128)(2,1)} %latent_ref.3), kind=kLoop, calls=%fused_computation | loop fusion | bytes 1048576 | tf_op jit(solution)/shard_map/slice | solution.py:236
  1.1 1.3 %collective-permute-start.1 = (bf16[1,256,512]{2,1,0:T(8,128)(2,1)S(1)}, bf16[1,256,512]{2,1,0:T(8,128)(2,1)S(1)}, u32[]{:S(2)}, u32[]{:S(2)}) collective-permute-start(bf16[1,256,512]{2,1,0:T(8,128)(2,1)S(1)} %get-tuple-element.15), channel_id=1, source_target_pairs={{1,0},{2,1},{3,2},{4,3},{5,4},{6,5},{7,6},{8,7},{9,8},{10,9},{11,1... | collective-permute-start | bytes 786440 | tf_op jit(solution)/shard_map/ppermute | solution.py:236
  2.4 3.0 %collective-permute-start = (bf16[1,256,512]{2,1,0:T(8,128)(2,1)S(1)}, bf16[1,256,512]{2,1,0:T(8,128)(2,1)S(1)}, u32[]{:S(2)}, u32[]{:S(2)}) collective-permute-start(bf16[1,256,512]{2,1,0:T(8,128)(2,1)S(1)} %get-tuple-element.16), channel_id=1, source_target_pairs={{0,1},{1,2},{2,3},{3,4},{4,5},{5,6},{6,7},{7,8},{8,9},{9,10},{10,1... | collective-permute-start | bytes 786440 | tf_op jit(solution)/shard_map/ppermute | solution.py:235
  5.4 0.0 copy-start.3
  5.4 1.0 %copy-done.3 = bf16[2,256,512]{2,1,0:T(8,128)(2,1)S(1)} copy-done((bf16[2,256,512]{2,1,0:T(8,128)(2,1)S(1)}, bf16[2,256,512]{2,1,0:T(8,128)(2,1)}, u32[]{:S(2)}) %copy-start.3) | copy-done | bytes 524312
  6.5 0.7 %stats.1 = f32[16,8,128]{2,1,0:T(8,128)} custom-call(bf16[2,256,512]{2,1,0:T(8,128)(2,1)S(1)} %copy-done.3), custom_call_target="tpu_custom_call" | custom-call | tf_op jit(solution)/shard_map/stats/pallas_call | solution.py:238
  7.2 7.9 %all-to-all-start = ((f32[16,8,128]{2,1,0:T(8,128)}), f32[16,8,128]{2,1,0:T(8,128)S(1)}, u32[]{:S(2)}, u32[]{:S(2)}) async-start(f32[16,8,128]{2,1,0:T(8,128)} %stats.1), calls=%async_computation | async-start | bytes 131072 | tf_op jit(solution)/shard_map/all_to_all | solution.py:246
  15.1 0.0 copy-start.7
  15.2 1.7 %copy-done.7 = bf16[4608,256]{1,0:T(8,128)(2,1)S(1)} copy-done((bf16[4608,256]{1,0:T(8,128)(2,1)S(1)}, bf16[4608,256]{1,0:T(8,128)(2,1)}, u32[]{:S(2)}) %copy-start.7) | copy-done | bytes 2359320
  16.8 0.7 %combine.1.weights_ref = bf16[4,2048,256]{2,1,0:T(8,128)(2,1)S(1)} custom-call(bf16[4608,256]{1,0:T(8,128)(2,1)S(1)} %copy-done.7), custom_call_target="tpu_custom_call" | custom-call | flops 4194304 | bytes 8388608 | tf_op jit(solution)/shard_map/combine/pallas_call | solution.py:248
  17.6 1.9 %copy-done = bf16[4,2048,256]{2,1,0:T(8,128)(2,1)} copy-done((bf16[4,2048,256]{2,1,0:T(8,128)(2,1)}, bf16[4,2048,256]{2,1,0:T(8,128)(2,1)S(1)}, u32[]{:S(2)}) %copy-start) | copy-done | bytes 4194328
  19.5 2.5 %all-to-all-done.stats_ref = f32[16,8,128]{2,1,0:T(8,128)S(1)} async-done(((f32[16,8,128]{2,1,0:T(8,128)}), f32[16,8,128]{2,1,0:T(8,128)S(1)}, u32[]{:S(2)}, u32[]{:S(2)}) %all-to-all-start) | async-done | bytes 65568 | tf_op jit(solution)/shard_map/all_to_all | solution.py:246
  22.0 0.0 collective-permute-done.1.down_ref
  22.0 0.0 collective-permute-done.up_ref
  22.1 2.2 %copy-done.1 = bf16[4,2048,256]{2,1,0:T(8,128)(2,1)S(1)} copy-done((bf16[4,2048,256]{2,1,0:T(8,128)(2,1)S(1)}, bf16[4,2048,256]{2,1,0:T(8,128)(2,1)}, u32[]{:S(2)}) %copy-start.1) | copy-done | bytes 4194328
  24.3 3.4 %hidden.1 = (bf16[4,256,1536]{2,1,0:T(8,128)(2,1)S(1)}, bf16[4,2,256,256]{3,2,1,0:T(8,128)(2,1)S(1)}, f32[16,8,128]{2,1,0:T(8,128)}) custom-call(f32[16,8,128]{2,1,0:T(8,128)S(1)} %all-to-all-done.stats_ref, bf16[1,256,512]{2,1,0:T(8,128)(2,1)S(1)} %collective-permute-done.up_ref, bf16[2,256,512]{2,1,0:T(8,128)(2,1)S(1)} %copy-done.4, ...), custom_call_target="tpu_custom_call" | custom-call | tf_op jit(solution)/shard_map/hidden/pallas_call | solution.py:258
  27.7 1.7 %copy-done.5 = bf16[4,256,1536]{2,1,0:T(8,128)(2,1)} copy-done((bf16[4,256,1536]{2,1,0:T(8,128)(2,1)}, bf16[4,256,1536]{2,1,0:T(8,128)(2,1)S(1)}, u32[]{:S(2)}) %copy-start.5) | copy-done | bytes 3145752
  29.4 3.5 %all-to-all-start.1 = ((f32[16,8,128]{2,1,0:T(8,128)}), f32[16,8,128]{2,1,0:T(8,128)S(1)}, u32[]{:S(2)}, u32[]{:S(2)}) async-start(f32[16,8,128]{2,1,0:T(8,128)} %get-tuple-element.10), calls=%async_computation.1 | async-start | bytes 131072 | tf_op jit(solution)/shard_map/all_to_all | solution.py:272
  32.9 2.2 %copy-done.2 = bf16[4,2048,256]{2,1,0:T(8,128)(2,1)S(1)} copy-done((bf16[4,2048,256]{2,1,0:T(8,128)(2,1)S(1)}, bf16[4,2048,256]{2,1,0:T(8,128)(2,1)}, u32[]{:S(2)}) %copy-start.2) | copy-done | bytes 4194328
  35.1 1.9 %copy-done.6 = bf16[4,256,1536]{2,1,0:T(8,128)(2,1)S(1)} copy-done((bf16[4,256,1536]{2,1,0:T(8,128)(2,1)S(1)}, bf16[4,256,1536]{2,1,0:T(8,128)(2,1)}, u32[]{:S(2)}) %copy-start.6) | copy-done | bytes 3145752
  37.0 0.9 %copy-done.9 = bf16[512,256]{1,0:T(8,128)(2,1)S(1)} copy-done((bf16[512,256]{1,0:T(8,128)(2,1)S(1)}, bf16[512,256]{1,0:T(8,128)(2,1)}, u32[]{:S(2)}) %copy-start.9) | copy-done | bytes 262168
  37.9 1.4 %border.1 = (bf16[2,2,256,256]{3,2,1,0:T(8,128)(2,1)S(1)}, f32[512,256]{1,0:T(8,128)S(1)}) custom-call(bf16[4,256,1536]{2,1,0:T(8,128)(2,1)S(1)} %copy-done.6, bf16[4,2048,256]{2,1,0:T(8,128)(2,1)S(1)} %copy-done.2, bf16[512,256]{1,0:T(8,128)(2,1)S(1)} %copy-done.9), custom_call_target="tpu_custom_call" | custom-call | flops 1258291200 | bytes 8388608 | tf_op jit(solution)/shard_map/border/pallas_call | solution.py:274
  39.3 0.4 %all-to-all-done.1.stats_ref = f32[16,8,128]{2,1,0:T(8,128)S(1)} async-done(((f32[16,8,128]{2,1,0:T(8,128)}), f32[16,8,128]{2,1,0:T(8,128)S(1)}, u32[]{:S(2)}, u32[]{:S(2)}) %all-to-all-start.1) | async-done | bytes 65568 | tf_op jit(solution)/shard_map/all_to_all | solution.py:272
  39.8 4.0 %output.1 = bf16[4,512,256]{2,1,0:T(8,128)(2,1)} custom-call(f32[16,8,128]{2,1,0:T(8,128)S(1)} %all-to-all-done.1.stats_ref, bf16[2,2,256,256]{3,2,1,0:T(8,128)(2,1)S(1)} %get-tuple-element.12.border_ref, bf16[4,2,256,256]{3,2,1,0:T(8,128)(2,1)S(1)} %get-tuple-element.13.hidden_ref, f32[1,256]{1,0:T(1,128)S(1)} %bitcast.6, f32[1,256]{1,0:T(1,128)S(1)} %bitcast.7, ...), custom_call_target="tpu_custom_call" | custom-call | tf_op jit(solution)/shard_map/output/pallas_call | solution.py:287
  (18 shorter events, 0.0 us)
Async XLA Ops:
  1.1 21.0 %collective-permute-start.1 = (bf16[1,256,512]{2,1,0:T(8,128)(2,1)S(1)}, bf16[1,256,512]{2,1,0:T(8,128)(2,1)S(1)}, u32[]{:S(2)}, u32[]{:S(2)}) collective-permute-start(bf16[1,256,512]{2,1,0:T(8,128)(2,1)S(1)} %get-tuple-element.15), channel_id=1, source_target_pairs={{1,0},{2,1},{3,2},{4,3},{5,4},{6,5},{7,6},{8,7},{9,8},{10,9},{11,1... | collective-permute-start | bytes 786440 | tf_op jit(solution)/shard_map/ppermute | solution.py:236
  2.4 19.7 %collective-permute-start = (bf16[1,256,512]{2,1,0:T(8,128)(2,1)S(1)}, bf16[1,256,512]{2,1,0:T(8,128)(2,1)S(1)}, u32[]{:S(2)}, u32[]{:S(2)}) collective-permute-start(bf16[1,256,512]{2,1,0:T(8,128)(2,1)S(1)} %get-tuple-element.16), channel_id=1, source_target_pairs={{0,1},{1,2},{2,3},{3,4},{4,5},{5,6},{6,7},{7,8},{8,9},{9,10},{10,1... | collective-permute-start | bytes 786440 | tf_op jit(solution)/shard_map/ppermute | solution.py:235
  5.4 1.0 %copy-start.3 = (bf16[2,256,512]{2,1,0:T(8,128)(2,1)S(1)}, bf16[2,256,512]{2,1,0:T(8,128)(2,1)}, u32[]{:S(2)}) copy-start(bf16[2,256,512]{2,1,0:T(8,128)(2,1)} %latent_ref.3) | copy-start | bytes 1572868
  7.2 14.8 %all-to-all-start = ((f32[16,8,128]{2,1,0:T(8,128)}), f32[16,8,128]{2,1,0:T(8,128)S(1)}, u32[]{:S(2)}, u32[]{:S(2)}) async-start(f32[16,8,128]{2,1,0:T(8,128)} %stats.1), calls=%async_computation | async-start | bytes 131072 | tf_op jit(solution)/shard_map/all_to_all | solution.py:246
  15.1 1.7 %copy-start.7 = (bf16[4608,256]{1,0:T(8,128)(2,1)S(1)}, bf16[4608,256]{1,0:T(8,128)(2,1)}, u32[]{:S(2)}) copy-start(bf16[4608,256]{1,0:T(8,128)(2,1)} %weight_ref.2) | copy-start | bytes 7077892
  16.8 5.2 %copy-start.4 = (bf16[2,256,512]{2,1,0:T(8,128)(2,1)S(1)}, bf16[2,256,512]{2,1,0:T(8,128)(2,1)}, u32[]{:S(2)}) copy-start(bf16[2,256,512]{2,1,0:T(8,128)(2,1)} %latent_ref.3) | copy-start | bytes 1572868
  16.8 5.2 %copy-start.10 = (f32[512]{0:T(512)S(1)}, f32[512]{0:T(512)}, u32[]{:S(2)}) copy-start(f32[512]{0:T(512)} %param.9) | copy-start | bytes 6148
  16.8 5.2 %copy-start.11 = (f32[512]{0:T(512)S(1)}, f32[512]{0:T(512)}, u32[]{:S(2)}) copy-start(f32[512]{0:T(512)} %param.10) | copy-start | bytes 6148
  17.6 1.9 %copy-start = (bf16[4,2048,256]{2,1,0:T(8,128)(2,1)}, bf16[4,2048,256]{2,1,0:T(8,128)(2,1)S(1)}, u32[]{:S(2)}) copy-start(bf16[4,2048,256]{2,1,0:T(8,128)(2,1)S(1)} %combine.1.weights_ref) | copy-start | bytes 12582916
  22.1 2.2 %copy-start.1 = (bf16[4,2048,256]{2,1,0:T(8,128)(2,1)S(1)}, bf16[4,2048,256]{2,1,0:T(8,128)(2,1)}, u32[]{:S(2)}) copy-start(bf16[4,2048,256]{2,1,0:T(8,128)(2,1)} %copy-done) | copy-start | bytes 12582916
  27.7 1.7 %copy-start.5 = (bf16[4,256,1536]{2,1,0:T(8,128)(2,1)}, bf16[4,256,1536]{2,1,0:T(8,128)(2,1)S(1)}, u32[]{:S(2)}) copy-start(bf16[4,256,1536]{2,1,0:T(8,128)(2,1)S(1)} %get-tuple-element.11.act_ref) | copy-start | bytes 9437188
  29.4 10.4 %all-to-all-start.1 = ((f32[16,8,128]{2,1,0:T(8,128)}), f32[16,8,128]{2,1,0:T(8,128)S(1)}, u32[]{:S(2)}, u32[]{:S(2)}) async-start(f32[16,8,128]{2,1,0:T(8,128)} %get-tuple-element.10), calls=%async_computation.1 | async-start | bytes 131072 | tf_op jit(solution)/shard_map/all_to_all | solution.py:272
  32.9 2.2 %copy-start.2 = (bf16[4,2048,256]{2,1,0:T(8,128)(2,1)S(1)}, bf16[4,2048,256]{2,1,0:T(8,128)(2,1)}, u32[]{:S(2)}) copy-start(bf16[4,2048,256]{2,1,0:T(8,128)(2,1)} %copy-done) | copy-start | bytes 12582916
  35.1 1.9 %copy-start.6 = (bf16[4,256,1536]{2,1,0:T(8,128)(2,1)S(1)}, bf16[4,256,1536]{2,1,0:T(8,128)(2,1)}, u32[]{:S(2)}) copy-start(bf16[4,256,1536]{2,1,0:T(8,128)(2,1)} %copy-done.5) | copy-start | bytes 9437188
  37.0 0.9 %copy-start.9 = (bf16[512,256]{1,0:T(8,128)(2,1)S(1)}, bf16[512,256]{1,0:T(8,128)(2,1)}, u32[]{:S(2)}) copy-start(bf16[512,256]{1,0:T(8,128)(2,1)} %skip_ref.1) | copy-start | bytes 786436
  37.9 1.8 %copy-start.8 = (bf16[2304,256]{1,0:T(8,128)(2,1)S(1)}, bf16[2304,256]{1,0:T(8,128)(2,1)}, u32[]{:S(2)}) copy-start(bf16[2304,256]{1,0:T(8,128)(2,1)} %weight_ref.3) | copy-start | bytes 3538948
  37.9 1.8 %copy-start.12 = (f32[256]{0:T(256)S(1)}, f32[256]{0:T(256)}, u32[]{:S(2)}) copy-start(f32[256]{0:T(256)} %param.12) | copy-start | bytes 3076
  37.9 1.8 %copy-start.13 = (f32[256]{0:T(256)S(1)}, f32[256]{0:T(256)}, u32[]{:S(2)}) copy-start(f32[256]{0:T(256)} %param.13) | copy-start | bytes 3076

commit v2 on v1

v2 whole, which is shorter than its diff:
```python
import functools

import jax
import jax.numpy as jnp
from jax import lax
from jax.experimental import pallas as pl
from jax.experimental.pallas import tpu as pltpu
from jax.sharding import PartitionSpec as P

GROUPS = 32
EPS = 1e-06
F32 = jnp.float32
BF16 = jnp.bfloat16
LANES = 128
PARTS = 4
VMEM = pltpu.VMEM


def vmem_spec():
    return pl.BlockSpec(memory_space=VMEM)


def in_hbm(values):
    return pltpu.with_memory_space_constraint(values, pltpu.HBM)


def params(limit_mib):
    return pltpu.CompilerParams(vmem_limit_bytes=limit_mib << 20)


def cost(flops, data):
    return pl.CostEstimate(flops=flops, bytes_accessed=data, transcendentals=0)


def stack_lanes(row):
    count = row.shape[1] // LANES
    return [row[:, i * LANES : (i + 1) * LANES] for i in range(count)]


def put_stats(out_ref, total, square):
    rows = stack_lanes(total) + stack_lanes(square)
    fill = 8 - len(rows)
    if fill:
        rows.append(jnp.zeros((fill, LANES), F32))
    tile = jnp.concatenate(rows, axis=0)
    out_ref[...] = jnp.broadcast_to(tile[None], out_ref.shape)


def get_affine(stats_ref, gain, shift, group_width, count):
    chans = gain.shape[1]
    half = chans // LANES
    total = jnp.sum(stats_ref[...], axis=0)
    left = lax.broadcasted_iota(jnp.int32, (LANES, LANES), 0) // group_width
    right = lax.broadcasted_iota(jnp.int32, (LANES, LANES), 1) // group_width
    same = (left == right).astype(F32)
    pooled = jnp.dot(total, same, preferred_element_type=F32, precision=lax.Precision.HIGHEST)
    scaled = pooled * (1.0 / count)
    center = jnp.concatenate([scaled[i : i + 1] for i in range(half)], axis=1)
    moment = jnp.concatenate([scaled[half + i : half + i + 1] for i in range(half)], axis=1)
    spread = jnp.maximum(moment - center * center, 0.0)
    scale = gain * lax.rsqrt(spread + EPS)
    return 0.5 * scale, 0.5 * (shift - center * scale)


def half_silu(values, scale, offset):
    halved = values * scale + offset
    return halved + halved * jnp.tanh(halved)


def shift_rows(values, step):
    size = values.shape[0]
    moved = pltpu.roll(values, step % size, 0)
    place = lax.broadcasted_iota(jnp.int32, (size, 1), 0)
    edge = 0 if step == 1 else size - 1
    return jnp.where(place == edge, 0.0, moved)


def stats_kernel(latent_ref, stats_ref, head_ref, tail_ref, held_ref, sems):
    rows = latent_ref.shape[0]
    copies = [
        pltpu.make_async_copy(latent_ref.at[row], held_ref.at[row], sems.at[row])
        for row in range(rows)
    ]
    for copy in copies:
        copy.start()
    total, square = 0.0, 0.0
    for row in range(rows):
        copies[row].wait()
        values = held_ref[row].astype(F32)
        total += jnp.sum(values, axis=0, keepdims=True)
        square += jnp.sum(values * values, axis=0, keepdims=True)
    put_stats(stats_ref, total, square)
    head_ref[0] = held_ref[0]
    tail_ref[0] = held_ref[rows - 1]


def combine_kernel(weight_ref, out_ref, held_ref, made_ref, in_sems, out_sems):
    step = 16
    chans = weight_ref.shape[1]
    width = chans // PARTS

    def pairs(taps):
        return (taps[0], taps[1] + taps[2]), (taps[0] + taps[1], taps[2])

    fetches, stores = [], []
    for index in range(PARTS):
        part = pl.ds(index * width, width)
        fetches.append(
            pltpu.make_async_copy(
                weight_ref.at[:, part, :], held_ref.at[:, part, :], in_sems.at[index]
            )
        )
        stores.append(
            pltpu.make_async_copy(
                made_ref.at[:, :, part, :], out_ref.at[:, :, part, :], out_sems.at[index]
            )
        )
    for fetch in fetches:
        fetch.start()
    for index in range(PARTS):
        fetches[index].wait()

        @pl.loop(0, width // step)
        def _(inner):
            part = pl.ds(pl.multiple_of(index * width + inner * step, step), step)
            columns = [
                pairs([held_ref[3 * a + b, part, :].astype(F32) for a in range(3)])
                for b in range(3)
            ]
            for row_phase in range(2):
                for row_tap in range(2):
                    across = pairs([columns[b][row_phase][row_tap] for b in range(3)])
                    for col_phase in range(2):
                        for col_tap in range(2):
                            made_ref[
                                2 * row_phase + col_phase, 2 * row_tap + col_tap, part, :
                            ] = across[col_phase][col_tap].astype(BF16)

        stores[index].start()
    for store in stores:
        store.wait()


def fill_act(out_ref, row, act):
    chans = act.shape[1]
    out_ref[row, :, 0:chans] = shift_rows(act, 1).astype(BF16)
    out_ref[row, :, chans : 2 * chans] = act.astype(BF16)
    out_ref[row, :, 2 * chans :] = shift_rows(act, -1).astype(BF16)


def first_conv(act_ref, weight_ref, col_phase, first, count):
    wide = act_ref.shape[2] // 3
    window = pl.ds(col_phase * wide, 2 * wide)
    lhs = jnp.concatenate(
        [
            act_ref[first + tap : first + tap + count, :, window].reshape(-1, 2 * wide)
            for tap in range(2)
        ],
        axis=1,
    )
    return jnp.dot(lhs, weight_ref[...], preferred_element_type=F32)


def fetch(weights_ref, held_ref, sems):
    copies = [
        pltpu.make_async_copy(weights_ref.at[phase], held_ref.at[phase], sems.at[phase])
        for phase in range(4)
    ]
    for copy in copies:
        copy.start()
    return copies


def hidden_kernel(
    count,
    axis_count,
    stats_ref,
    up_ref,
    latent_ref,
    down_ref,
    gain_ref,
    shift_ref,
    weights_ref,
    act_ref,
    hidden_ref,
    out_ref,
    shifted_ref,
    held_ref,
    sems,
):
    copies = fetch(weights_ref, held_ref, sems)
    rows, cols, chans = latent_ref.shape
    scale, offset = get_affine(stats_ref, gain_ref[...], shift_ref[...], chans // GROUPS, count)
    place = lax.axis_index("rows")
    for row in range(rows + 2):
        if row == 0:
            source, keep = up_ref[0], place > 0
        elif row == rows + 1:
            source, keep = down_ref[0], place < axis_count - 1
        else:
            source, keep = latent_ref[row - 1], None
        act = half_silu(source.astype(F32), scale, offset)
        if keep is not None:
            act = act * keep.astype(F32)
        act_ref[row] = act.astype(BF16)
        fill_act(shifted_ref, row, act)
    totals, squares = [], []
    for row_phase in range(2):
        for col_phase in range(2):
            phase = 2 * row_phase + col_phase
            copies[phase].wait()
            found = first_conv(shifted_ref, held_ref.at[phase], col_phase, row_phase, rows)
            found = found.astype(BF16)
            for row in range(rows):
                hidden_ref[2 * row + row_phase, col_phase] = found[row * cols : (row + 1) * cols]
            wide = found.astype(F32)
            totals.append(jnp.sum(wide, axis=0, keepdims=True))
            squares.append(jnp.sum(wide * wide, axis=0, keepdims=True))
    put_stats(out_ref, sum(totals[1:], totals[0]), sum(squares[1:], squares[0]))


def border_kernel(
    act_ref,
    weights_ref,
    skip_ref,
    border_ref,
    skipped_ref,
    shifted_ref,
    held_ref,
    skip_held_ref,
    sems,
    skip_sem,
):
    skip_copy = pltpu.make_async_copy(skip_ref, skip_held_ref, skip_sem)
    skip_copy.start()
    copies = fetch(weights_ref, held_ref, sems)
    total, cols, chans = act_ref.shape
    rows = total - 2
    for row in range(total):
        fill_act(shifted_ref, row, act_ref[row].astype(F32))
    skip_copy.wait()
    skipped_ref[...] = jnp.dot(
        act_ref[1 : 1 + rows].reshape(-1, chans), skip_held_ref[...], preferred_element_type=F32
    )
    for row_phase in range(2):
        side, first = (1, rows) if row_phase == 0 else (0, 0)
        for col_phase in range(2):
            phase = 2 * row_phase + col_phase
            copies[phase].wait()
            border_ref[side, col_phase] = first_conv(
                shifted_ref, held_ref.at[phase], col_phase, first, 1
            ).astype(BF16)


def output_kernel(
    count,
    axis_count,
    stats_ref,
    border_ref,
    hidden_ref,
    gain_ref,
    shift_ref,
    weight_ref,
    skipped_ref,
    out_ref,
    mid_ref,
    mixed_ref,
    done_ref,
    held_ref,
    sems,
    held_sem,
):
    fetched = pltpu.make_async_copy(weight_ref, held_ref, held_sem)
    fetched.start()
    rows, _, cols, chans = hidden_ref.shape
    scale, offset = get_affine(stats_ref, gain_ref[...], shift_ref[...], chans // GROUPS, count)
    place = lax.axis_index("rows")
    for row in range(rows + 2):
        pair = []
        for phase in range(2):
            if row == 0:
                source, keep = border_ref[0, phase], place > 0
            elif row == rows + 1:
                source, keep = border_ref[1, phase], place < axis_count - 1
            else:
                source, keep = hidden_ref[row - 1, phase], None
            value = half_silu(source.astype(F32), scale, offset)
            if keep is not None:
                value = value * keep.astype(F32)
            pair.append(value)
        even, odd = pair
        mid_ref[row, :, 0:chans] = shift_rows(odd, 1).astype(BF16)
        mid_ref[row, :, chans : 2 * chans] = even.astype(BF16)
        mid_ref[row, :, 2 * chans : 3 * chans] = odd.astype(BF16)
        mid_ref[row, :, 3 * chans :] = shift_rows(even, -1).astype(BF16)
    fetched.wait()
    copies = []
    for row in range(rows):
        base = skipped_ref[pl.ds((row // 2) * cols, cols), :]
        for phase in range(2):
            lhs = jnp.concatenate(
                [mid_ref[row + tap, :, phase * chans : (phase + 3) * chans] for tap in range(3)],
                axis=1,
            )
            found = base + jnp.dot(lhs, held_ref[...], preferred_element_type=F32)
            for part in range(chans // LANES):
                mixed_ref[part, pl.ds(phase, cols, stride=2), :] = found[
                    :, part * LANES : (part + 1) * LANES
                ]
        for part in range(chans // LANES):
            done_ref[row, :, part * LANES : (part + 1) * LANES] = mixed_ref[part].astype(BF16)
        copy = pltpu.make_async_copy(done_ref.at[row], out_ref.at[row], sems.at[row])
        copy.start()
        copies.append(copy)
    for copy in copies:
        copy.wait()


def body(latent, gain_in, shift_in, conv_in, gain_mid, shift_mid, conv_mid, skip_weight):
    axis = "rows"
    peers = lax.axis_size(axis)
    rows, cols, chans = latent.shape
    outs = conv_in.shape[1]
    ends = peers - 1
    taken = vmem_spec()
    far = pl.BlockSpec(memory_space=pltpu.HBM)
    dma = pltpu.SemaphoreType.DMA
    whole = jax.ShapeDtypeStruct

    with jax.named_scope("stats"):
        stats, head, tail = pl.pallas_call(
            stats_kernel,
            out_shape=(
                whole((peers, 8, LANES), F32),
                whole((1, cols, chans), BF16),
                whole((1, cols, chans), BF16),
            ),
            in_specs=[far],
            out_specs=(taken,) * 3,
            scratch_shapes=[VMEM(latent.shape, BF16), dma((rows,))],
            compiler_params=params(16),
            name="stats",
        )(in_hbm(latent))
    with jax.named_scope("exchange_in"):
        stats = lax.all_to_all(stats, axis, 0, 0)
    with jax.named_scope("halo"):
        up = lax.ppermute(tail, axis, [(i, i + 1) for i in range(ends)])
        down = lax.ppermute(head, axis, [(i + 1, i) for i in range(ends)])

    with jax.named_scope("combine"):
        weights = pl.pallas_call(
            combine_kernel,
            out_shape=pltpu.HBM((4, 4, chans, outs), BF16),
            in_specs=[far],
            out_specs=far,
            scratch_shapes=[
                VMEM((9, chans, outs), BF16),
                VMEM((4, 4, chans, outs), BF16),
                dma((PARTS,)),
                dma((PARTS,)),
            ],
            compiler_params=params(16),
            cost_estimate=cost(4 << 20, 8 << 20),
            name="combine",
        )(in_hbm(conv_in.reshape(9, chans, outs))).reshape(4, 4 * chans, outs)

    with jax.named_scope("hidden"):
        act, hidden, stats_mid = pl.pallas_call(
            functools.partial(
                hidden_kernel, float(rows * cols * (chans // GROUPS) * peers), peers
            ),
            out_shape=(
                whole((rows + 2, cols, chans), BF16),
                whole((2 * rows, 2, cols, outs), BF16),
                whole((peers, 8, LANES), F32),
            ),
            in_specs=[taken] * 6 + [far],
            out_specs=(taken,) * 3,
            scratch_shapes=[
                VMEM((rows + 2, cols, 3 * chans), BF16),
                VMEM((4, 4 * chans, outs), BF16),
                dma((4,)),
            ],
            compiler_params=params(24),
            name="hidden",
        )(stats, up, latent, down, gain_in.reshape(1, -1), shift_in.reshape(1, -1), in_hbm(weights))
    with jax.named_scope("exchange_mid"):
        stats_mid = lax.all_to_all(stats_mid, axis, 0, 0)

    with jax.named_scope("border"):
        border, skipped = pl.pallas_call(
            border_kernel,
            out_shape=(
                whole((2, 2, cols, outs), BF16),
                whole((rows * cols, outs), F32),
            ),
            in_specs=[taken, far, far],
            out_specs=(taken,) * 2,
            scratch_shapes=[
                VMEM((rows + 2, cols, 3 * chans), BF16),
                VMEM((4, 4 * chans, outs), BF16),
                VMEM((chans, outs), BF16),
                dma((4,)),
                dma,
            ],
            compiler_params=params(24),
            cost_estimate=cost(1200 << 20, 8 << 20),
            name="border",
        )(act, in_hbm(weights), in_hbm(skip_weight))

    with jax.named_scope("output"):
        return pl.pallas_call(
            functools.partial(
                output_kernel, float(4 * rows * cols * (outs // GROUPS) * peers), peers
            ),
            out_shape=whole((2 * rows, 2 * cols, outs), BF16),
            in_specs=[taken] * 5 + [far, taken],
            out_specs=far,
            scratch_shapes=[
                VMEM((2 * rows + 2, cols, 4 * outs), BF16),
                VMEM((outs // LANES, 2 * cols, LANES), F32),
                VMEM((2 * rows, 2 * cols, outs), BF16),
                VMEM(conv_mid.shape, BF16),
                dma((2 * rows,)),
                dma,
            ],
            compiler_params=params(24),
            name="output",
        )(
            stats_mid,
            border,
            hidden,
            gain_mid.reshape(1, -1),
            shift_mid.reshape(1, -1),
            in_hbm(conv_mid),
            skipped,
        )


def solution(mesh):
    placed = (P(("groups", "rows"), None, None), P(), P(), P(), P(), P(), P(), P())
    return jax.shard_map(
        body,
        mesh=mesh,
        in_specs=placed,
        out_specs=P(("groups", "rows"), None, None),
        check_vma=False,
    )
```

time: 44.3 us -> 44.2 us (level)
  local copies, waits for them, and re-layouts: 14.6 us -> 0.03 us
  Pallas kernels: 10.3 us -> 21.8 us
  waiting for transfers between devices: 2.99 us -> 5.4 us
  starting transfers between devices: 15.8 us -> 16.5 us
    unnamed x28 -> x10, local copies, waits for them, and re-layouts: 13.5 us -> 0.03 us
    pallas_call x3, Pallas kernels: 2.85 us -> 10 us  [the longest x1 5.01 us: body(): pl.pallas_call(border_kernel, out_shape=(whole((2, 2, cols, outs), BF16),...]
    pallas_call x1, Pallas kernels: 3.43 us -> 6.9 us  [body(): pl.pallas_call(functools.partial(hidden_kernel, float(rows * cols * (chan...]
    all_to_all x1, waiting for transfers between devices: 0.45 us -> 1.82 us  [body(): stats_mid = lax.all_to_all(stats_mid, axis, 0, 0)]
    all_to_all x1, starting transfers between devices: 7.94 us -> 9.26 us  [body(): stats = lax.all_to_all(stats, axis, 0, 0)]
    slice x1 -> x0, local copies, waits for them, and re-layouts: 1.06 us -> none  [body(): down = lax.ppermute(latent[:1], axis, [(i + 1, i) for i in range(ends)])]
    all_to_all x1, waiting for transfers between devices: 2.54 us -> 3.57 us  [body(): stats = lax.all_to_all(stats, axis, 0, 0)]
    pallas_call x1, Pallas kernels: 4.01 us -> 4.84 us  [body(): pl.pallas_call(functools.partial(output_kernel, float(4 * rows * cols * (...]
  transfers between devices with their start and end apart: 4 -> 4, of which waited for: 2 -> 2; matrix products, arithmetic and copies ran while one was open for 0% -> 0% of each run, Pallas kernels for 6% -> 19%
where the time goes in v2:
time: 44.2 us; the launch traced here: 43.8 us
  Pallas kernels  21.8 us (49%)
  starting transfers between devices  16.5 us (37%)
  waiting for transfers between devices  5.4 us (12%)
    all_to_all x1, starting transfers between devices, body(): stats = lax.all_to_all(stats, axis, 0, 0)  9.26 us
    pallas_call x1, Pallas kernels, body(): pl.pallas_call(functools.partial(hidden_kernel, float(rows * cols * (chan...  6.9 us
    pallas_call x1, Pallas kernels, body(): pl.pallas_call(border_kernel, out_shape=(whole((2, 2, cols, outs), BF16),...  5.01 us
    pallas_call x1, Pallas kernels, body(): pl.pallas_call(functools.partial(output_kernel, float(4 * rows * cols * (...  4.84 us
    all_to_all x1, waiting for transfers between devices, body(): stats = lax.all_to_all(stats, axis, 0, 0)  3.57 us
    all_to_all x1, starting transfers between devices, body(): stats_mid = lax.all_to_all(stats_mid, axis, 0, 0)  3.51 us
    pallas_call x1, Pallas kernels, body(): pl.pallas_call(combine_kernel, out_shape=pltpu.HBM((4, 4, chans, outs), B...  3.28 us
    ppermute x1, starting transfers between devices, body(): up = lax.ppermute(tail, axis, [(i, i + 1) for i in range(ends)])  2.41 us
  transfers between devices with their start and end apart: 4, of which 2 were waited for; matrix products, arithmetic and copies ran while one was open for 0% of the time, Pallas kernels for 19%

profile of v2, /device:TPU:0, one launch (start us, length us, event | category | flops | bytes accessed | tf_op | source)
XLA Modules:
  0.0 43.8 jit_solution(918088064433445626)
XLA Ops:
  0.0 1.7 %stats.1 = (f32[16,8,128]{2,1,0:T(8,128)}, bf16[1,256,512]{2,1,0:T(8,128)(2,1)S(1)}, bf16[1,256,512]{2,1,0:T(8,128)(2,1)S(1)}) custom-call(bf16[2,256,512]{2,1,0:T(8,128)(2,1)} %latent_ref.3), custom_call_target="tpu_custom_call" | custom-call | tf_op jit(solution)/shard_map/stats/stats/pallas_call | solution.py:331
  1.8 2.4 %collective-permute-start = (bf16[1,256,512]{2,1,0:T(8,128)(2,1)S(1)}, bf16[1,256,512]{2,1,0:T(8,128)(2,1)S(1)}, u32[]{:S(2)}, u32[]{:S(2)}) collective-permute-start(bf16[1,256,512]{2,1,0:T(8,128)(2,1)S(1)} %get-tuple-element.14), channel_id=1, source_target_pairs={{0,1},{1,2},{2,3},{3,4},{4,5},{5,6},{6,7},{7,8},{8,9},{9,10},{10,1... | collective-permute-start | bytes 786440 | tf_op jit(solution)/shard_map/halo/ppermute | solution.py:347
  4.2 1.3 %collective-permute-start.1 = (bf16[1,256,512]{2,1,0:T(8,128)(2,1)S(1)}, bf16[1,256,512]{2,1,0:T(8,128)(2,1)S(1)}, u32[]{:S(2)}, u32[]{:S(2)}) collective-permute-start(bf16[1,256,512]{2,1,0:T(8,128)(2,1)S(1)} %get-tuple-element.15), channel_id=1, source_target_pairs={{1,0},{2,1},{3,2},{4,3},{5,4},{6,5},{7,6},{8,7},{9,8},{10,9},{11,1... | collective-permute-start | bytes 786440 | tf_op jit(solution)/shard_map/halo/ppermute | solution.py:348
  5.5 9.3 %all-to-all-start = ((f32[16,8,128]{2,1,0:T(8,128)}), f32[16,8,128]{2,1,0:T(8,128)S(1)}, u32[]{:S(2)}, u32[]{:S(2)}) async-start(f32[16,8,128]{2,1,0:T(8,128)} %get-tuple-element.13), calls=%async_computation | async-start | bytes 131072 | tf_op jit(solution)/shard_map/exchange_in/all_to_all | solution.py:345
  14.7 0.0 copy-start
  14.8 0.0 copy-start.1
  14.8 0.0 copy-start.2
  14.8 3.3 %combine.1 = bf16[4,4,512,256]{3,2,1,0:T(8,128)(2,1)} custom-call(bf16[9,512,256]{2,1,0:T(8,128)(2,1)} %bitcast.12), custom_call_target="tpu_custom_call" | custom-call | flops 4194304 | bytes 8388608 | tf_op jit(solution)/shard_map/combine/combine/pallas_call | solution.py:351
  18.1 3.6 %all-to-all-done.stats_ref = f32[16,8,128]{2,1,0:T(8,128)S(1)} async-done(((f32[16,8,128]{2,1,0:T(8,128)}), f32[16,8,128]{2,1,0:T(8,128)S(1)}, u32[]{:S(2)}, u32[]{:S(2)}) %all-to-all-start) | async-done | bytes 65568 | tf_op jit(solution)/shard_map/exchange_in/all_to_all | solution.py:345
  21.6 0.0 collective-permute-done.up_ref
  21.6 0.0 collective-permute-done.1.down_ref
  21.6 0.0 copy-done
  21.6 0.0 copy-done.1
  21.7 0.0 copy-done.2
  21.7 6.9 %hidden.1 = (bf16[4,256,512]{2,1,0:T(8,128)(2,1)S(1)}, bf16[4,2,256,256]{3,2,1,0:T(8,128)(2,1)S(1)}, f32[16,8,128]{2,1,0:T(8,128)}) custom-call(f32[16,8,128]{2,1,0:T(8,128)S(1)} %all-to-all-done.stats_ref, bf16[1,256,512]{2,1,0:T(8,128)(2,1)S(1)} %collective-permute-done.up_ref, bf16[2,256,512]{2,1,0:T(8,128)(2,1)S(1)} %copy-done, ...), custom_call_target="tpu_custom_call" | custom-call | tf_op jit(solution)/shard_map/hidden/hidden/pallas_call | solution.py:368
  28.6 3.5 %all-to-all-start.1 = ((f32[16,8,128]{2,1,0:T(8,128)}), f32[16,8,128]{2,1,0:T(8,128)S(1)}, u32[]{:S(2)}, u32[]{:S(2)}) async-start(f32[16,8,128]{2,1,0:T(8,128)} %get-tuple-element.16), calls=%async_computation.1 | async-start | bytes 131072 | tf_op jit(solution)/shard_map/exchange_mid/all_to_all | solution.py:388
  32.1 0.0 copy-start.3
  32.1 0.0 copy-start.4
  32.1 5.0 %border.1 = (bf16[2,2,256,256]{3,2,1,0:T(8,128)(2,1)S(1)}, f32[512,256]{1,0:T(8,128)S(1)}) custom-call(bf16[4,256,512]{2,1,0:T(8,128)(2,1)S(1)} %get-tuple-element.17.act_ref, bf16[4,2048,256]{2,1,0:T(8,128)(2,1)} %bitcast.11, bf16[512,256]{1,0:T(8,128)(2,1)} %skip_ref.1), custom_call_target="tpu_custom_call" | custom-call | flops 1258291200 | bytes 8388608 | tf_op jit(solution)/shard_map/border/border/pallas_call | solution.py:391
  37.1 1.8 %all-to-all-done.1.stats_ref = f32[16,8,128]{2,1,0:T(8,128)S(1)} async-done(((f32[16,8,128]{2,1,0:T(8,128)}), f32[16,8,128]{2,1,0:T(8,128)S(1)}, u32[]{:S(2)}, u32[]{:S(2)}) %all-to-all-start.1) | async-done | bytes 65568 | tf_op jit(solution)/shard_map/exchange_mid/all_to_all | solution.py:388
  39.0 0.0 copy-done.3
  39.0 0.0 copy-done.4
  39.0 4.8 %output.1 = bf16[4,512,256]{2,1,0:T(8,128)(2,1)} custom-call(f32[16,8,128]{2,1,0:T(8,128)S(1)} %all-to-all-done.1.stats_ref, bf16[2,2,256,256]{3,2,1,0:T(8,128)(2,1)S(1)} %get-tuple-element.18.border_ref, bf16[4,2,256,256]{3,2,1,0:T(8,128)(2,1)S(1)} %get-tuple-element.19.hidden_ref, f32[1,256]{1,0:T(1,128)S(1)} %bitcast.8, f32[1,256]{1,0:T(1,128)S(1)} %bitcast.9, ...), custom_call_target="tpu_custom_call" | custom-call | tf_op jit(solution)/shard_map/output/output/pallas_call | solution.py:412
Async XLA Ops:
  1.8 19.9 %collective-permute-start = (bf16[1,256,512]{2,1,0:T(8,128)(2,1)S(1)}, bf16[1,256,512]{2,1,0:T(8,128)(2,1)S(1)}, u32[]{:S(2)}, u32[]{:S(2)}) collective-permute-start(bf16[1,256,512]{2,1,0:T(8,128)(2,1)S(1)} %get-tuple-element.14), channel_id=1, source_target_pairs={{0,1},{1,2},{2,3},{3,4},{4,5},{5,6},{6,7},{7,8},{8,9},{9,10},{10,1... | collective-permute-start | bytes 786440 | tf_op jit(solution)/shard_map/halo/ppermute | solution.py:347
  4.2 17.5 %collective-permute-start.1 = (bf16[1,256,512]{2,1,0:T(8,128)(2,1)S(1)}, bf16[1,256,512]{2,1,0:T(8,128)(2,1)S(1)}, u32[]{:S(2)}, u32[]{:S(2)}) collective-permute-start(bf16[1,256,512]{2,1,0:T(8,128)(2,1)S(1)} %get-tuple-element.15), channel_id=1, source_target_pairs={{1,0},{2,1},{3,2},{4,3},{5,4},{6,5},{7,6},{8,7},{9,8},{10,9},{11,1... | collective-permute-start | bytes 786440 | tf_op jit(solution)/shard_map/halo/ppermute | solution.py:348
  5.5 16.2 %all-to-all-start = ((f32[16,8,128]{2,1,0:T(8,128)}), f32[16,8,128]{2,1,0:T(8,128)S(1)}, u32[]{:S(2)}, u32[]{:S(2)}) async-start(f32[16,8,128]{2,1,0:T(8,128)} %get-tuple-element.13), calls=%async_computation | async-start | bytes 131072 | tf_op jit(solution)/shard_map/exchange_in/all_to_all | solution.py:345
  14.7 6.9 %copy-start = (bf16[2,256,512]{2,1,0:T(8,128)(2,1)S(1)}, bf16[2,256,512]{2,1,0:T(8,128)(2,1)}, u32[]{:S(2)}) copy-start(bf16[2,256,512]{2,1,0:T(8,128)(2,1)} %latent_ref.3) | copy-start | bytes 1572868
  14.8 6.9 %copy-start.1 = (f32[512]{0:T(512)S(1)}, f32[512]{0:T(512)}, u32[]{:S(2)}) copy-start(f32[512]{0:T(512)} %param.9) | copy-start | bytes 6148
  14.8 6.9 %copy-start.2 = (f32[512]{0:T(512)S(1)}, f32[512]{0:T(512)}, u32[]{:S(2)}) copy-start(f32[512]{0:T(512)} %param.10) | copy-start | bytes 6148
  28.6 10.4 %all-to-all-start.1 = ((f32[16,8,128]{2,1,0:T(8,128)}), f32[16,8,128]{2,1,0:T(8,128)S(1)}, u32[]{:S(2)}, u32[]{:S(2)}) async-start(f32[16,8,128]{2,1,0:T(8,128)} %get-tuple-element.16), calls=%async_computation.1 | async-start | bytes 131072 | tf_op jit(solution)/shard_map/exchange_mid/all_to_all | solution.py:388
  32.1 6.9 %copy-start.3 = (f32[256]{0:T(256)S(1)}, f32[256]{0:T(256)}, u32[]{:S(2)}) copy-start(f32[256]{0:T(256)} %param.12) | copy-start | bytes 3076
  32.1 6.9 %copy-start.4 = (f32[256]{0:T(256)S(1)}, f32[256]{0:T(256)}, u32[]{:S(2)}) copy-start(f32[256]{0:T(256)} %param.13) | copy-start | bytes 3076

commit v3 on v2

v3 whole, which is shorter than its diff:
```python
import functools

import jax
import jax.numpy as jnp
from jax import lax
from jax.experimental import pallas as pl
from jax.experimental.pallas import tpu as pltpu
from jax.sharding import PartitionSpec as P

GROUPS = 32
EPS = 1e-06
F32 = jnp.float32
BF16 = jnp.bfloat16
LANES = 128
VMEM = pltpu.VMEM


def vmem_spec():
    return pl.BlockSpec(memory_space=VMEM)


def in_hbm(values):
    return pltpu.with_memory_space_constraint(values, pltpu.HBM)


def params(limit_mib):
    return pltpu.CompilerParams(vmem_limit_bytes=limit_mib << 20)


def cost(flops, data):
    return pl.CostEstimate(flops=flops, bytes_accessed=data, transcendentals=0)


def stack_lanes(row):
    count = row.shape[1] // LANES
    return [row[:, i * LANES : (i + 1) * LANES] for i in range(count)]


def put_stats(out_ref, total, square):
    rows = stack_lanes(total) + stack_lanes(square)
    fill = 8 - len(rows)
    if fill:
        rows.append(jnp.zeros((fill, LANES), F32))
    tile = jnp.concatenate(rows, axis=0)
    out_ref[...] = jnp.broadcast_to(tile[None], out_ref.shape)


def get_affine(stats_ref, gain, shift, group_width, count):
    chans = gain.shape[1]
    half = chans // LANES
    total = jnp.sum(stats_ref[...], axis=0)
    left = lax.broadcasted_iota(jnp.int32, (LANES, LANES), 0) // group_width
    right = lax.broadcasted_iota(jnp.int32, (LANES, LANES), 1) // group_width
    same = (left == right).astype(F32)
    pooled = jnp.dot(total, same, preferred_element_type=F32, precision=lax.Precision.HIGHEST)
    scaled = pooled * (1.0 / count)
    center = jnp.concatenate([scaled[i : i + 1] for i in range(half)], axis=1)
    moment = jnp.concatenate([scaled[half + i : half + i + 1] for i in range(half)], axis=1)
    spread = jnp.maximum(moment - center * center, 0.0)
    scale = gain * lax.rsqrt(spread + EPS)
    return 0.5 * scale, 0.5 * (shift - center * scale)


def half_silu(values, scale, offset):
    halved = values * scale + offset
    return halved + halved * jnp.tanh(halved)


def shift_rows(values, step):
    size = values.shape[0]
    moved = pltpu.roll(values, step % size, 0)
    place = lax.broadcasted_iota(jnp.int32, (size, 1), 0)
    edge = 0 if step == 1 else size - 1
    return jnp.where(place == edge, 0.0, moved)


def stats_kernel(latent_ref, stats_ref, head_ref, tail_ref, held_ref, sems):
    rows = latent_ref.shape[0]
    copies = [
        pltpu.make_async_copy(latent_ref.at[row], held_ref.at[row], sems.at[row])
        for row in range(rows)
    ]
    for copy in copies:
        copy.start()
    total, square = 0.0, 0.0
    for row in range(rows):
        copies[row].wait()
        values = held_ref[row].astype(F32)
        total += jnp.sum(values, axis=0, keepdims=True)
        square += jnp.sum(values * values, axis=0, keepdims=True)
    put_stats(stats_ref, total, square)
    head_ref[0] = held_ref[0]
    tail_ref[0] = held_ref[rows - 1]


def fetch_all(pairs, sems):
    copies = [
        pltpu.make_async_copy(source, target, sems.at[index])
        for index, (source, target) in enumerate(pairs)
    ]
    for copy in copies:
        copy.start()
    return copies


def hidden_kernel(
    count,
    axis_count,
    stats_ref,
    up_ref,
    latent_ref,
    down_ref,
    gain_ref,
    shift_ref,
    weight_ref,
    skip_ref,
    hidden_ref,
    out_ref,
    skipped_ref,
    act_ref,
    tap_ref,
    gains_ref,
    rows_ref,
    taps_ref,
    skips_ref,
    sems,
):
    rows, cols, chans = latent_ref.shape
    pairs = [(gain_ref, gains_ref.at[0]), (shift_ref, gains_ref.at[1]), (latent_ref, rows_ref)]
    order = [0, 1, 2, 6, 7, 8, 3, 4, 5]
    for tap in order:
        pairs.append((weight_ref.at[pl.ds(tap * chans, chans), :], taps_ref.at[tap]))
    pairs.append((skip_ref, skips_ref))
    copies = fetch_all(pairs, sems)
    copies[0].wait()
    copies[1].wait()
    scale, offset = get_affine(stats_ref, gains_ref[0], gains_ref[1], chans // GROUPS, count)
    place = lax.axis_index("rows")
    for row in [0, rows + 1] + list(range(1, rows + 1)):
        if row == 0:
            source, keep = up_ref[0], place > 0
        elif row == rows + 1:
            source, keep = down_ref[0], place < axis_count - 1
        else:
            if row == 1:
                copies[2].wait()
            source, keep = rows_ref[row - 1], None
        act = half_silu(source.astype(F32), scale, offset)
        if keep is not None:
            act = act * keep.astype(F32)
        act_ref[pl.ds(row * cols, cols), :] = act.astype(BF16)

    total_rows = 2 * rows + 2
    sources = [[(row + tap - 2) // 2 + 1 for tap in range(3)] for row in range(total_rows)]
    for index, tap in enumerate(order):
        copies[3 + index].wait()
        used = [source[tap // 3] for source in sources]
        first, last = min(used), max(used)
        part = pl.ds(first * cols, (last + 1 - first) * cols)
        tap_ref[tap, part, :] = jnp.dot(
            act_ref[part, :],
            taps_ref[tap],
            preferred_element_type=F32,
        )
    copies[12].wait()
    middle = act_ref[cols : (rows + 1) * cols, :]
    skipped_ref[...] = jnp.dot(middle, skips_ref[...], preferred_element_type=F32)

    totals, squares = [], []
    for row in range(total_rows):
        left, center, right = (
            sum(
                tap_ref[3 * a + b, pl.ds(sources[row][a] * cols, cols), :] for a in range(3)
            )
            for b in range(3)
        )
        pair = (
            shift_rows(left, 1) + (center + right),
            (left + center) + shift_rows(right, -1),
        )
        for phase in range(2):
            found = pair[phase].astype(BF16)
            hidden_ref[row, phase] = found
            if 0 < row < total_rows - 1:
                wide = found.astype(F32)
                totals.append(jnp.sum(wide, axis=0, keepdims=True))
                squares.append(jnp.sum(wide * wide, axis=0, keepdims=True))
    put_stats(out_ref, sum(totals[1:], totals[0]), sum(squares[1:], squares[0]))


def output_kernel(
    count,
    axis_count,
    stats_ref,
    hidden_ref,
    gain_ref,
    shift_ref,
    weight_ref,
    skipped_ref,
    out_ref,
    mid_ref,
    mixed_ref,
    done_ref,
    held_ref,
    gains_ref,
    sems,
    in_sems,
):
    fetches = fetch_all(
        [(gain_ref, gains_ref.at[0]), (shift_ref, gains_ref.at[1]), (weight_ref, held_ref)],
        in_sems,
    )
    total_rows, _, cols, chans = hidden_ref.shape
    rows = total_rows - 2
    fetches[0].wait()
    fetches[1].wait()
    scale, offset = get_affine(stats_ref, gains_ref[0], gains_ref[1], chans // GROUPS, count)
    place = lax.axis_index("rows")
    for row in range(rows + 2):
        pair = []
        keep = None
        if row == 0:
            keep = place > 0
        elif row == rows + 1:
            keep = place < axis_count - 1
        for phase in range(2):
            value = half_silu(hidden_ref[row, phase].astype(F32), scale, offset)
            if keep is not None:
                value = value * keep.astype(F32)
            pair.append(value)
        even, odd = pair
        mid_ref[row, :, 0:chans] = shift_rows(odd, 1).astype(BF16)
        mid_ref[row, :, chans : 2 * chans] = even.astype(BF16)
        mid_ref[row, :, 2 * chans : 3 * chans] = odd.astype(BF16)
        mid_ref[row, :, 3 * chans :] = shift_rows(even, -1).astype(BF16)
    fetches[2].wait()
    copies = []
    for row in range(rows):
        base = skipped_ref[pl.ds((row // 2) * cols, cols), :]
        for phase in range(2):
            lhs = jnp.concatenate(
                [mid_ref[row + tap, :, phase * chans : (phase + 3) * chans] for tap in range(3)],
                axis=1,
            )
            found = base + jnp.dot(lhs, held_ref[...], preferred_element_type=F32)
            for part in range(chans // LANES):
                mixed_ref[part, pl.ds(phase, cols, stride=2), :] = found[
                    :, part * LANES : (part + 1) * LANES
                ]
        for part in range(chans // LANES):
            done_ref[row, :, part * LANES : (part + 1) * LANES] = mixed_ref[part].astype(BF16)
        copy = pltpu.make_async_copy(done_ref.at[row], out_ref.at[row], sems.at[row])
        copy.start()
        copies.append(copy)
    for copy in copies:
        copy.wait()


def body(latent, gain_in, shift_in, conv_in, gain_mid, shift_mid, conv_mid, skip_weight):
    axis = "rows"
    peers = lax.axis_size(axis)
    rows, cols, chans = latent.shape
    outs = conv_in.shape[1]
    ends = peers - 1
    taken = vmem_spec()
    far = pl.BlockSpec(memory_space=pltpu.HBM)
    dma = pltpu.SemaphoreType.DMA
    whole = jax.ShapeDtypeStruct

    with jax.named_scope("stats"):
        stats, head, tail = pl.pallas_call(
            stats_kernel,
            out_shape=(
                whole((peers, 8, LANES), F32),
                whole((1, cols, chans), BF16),
                whole((1, cols, chans), BF16),
            ),
            in_specs=[far],
            out_specs=(taken,) * 3,
            scratch_shapes=[VMEM(latent.shape, BF16), dma((rows,))],
            compiler_params=params(16),
            name="stats",
        )(in_hbm(latent))
    with jax.named_scope("exchange_in"):
        stats = lax.all_to_all(stats, axis, 0, 0)
    with jax.named_scope("halo"):
        up = lax.ppermute(tail, axis, [(i, i + 1) for i in range(ends)])
        down = lax.ppermute(head, axis, [(i + 1, i) for i in range(ends)])

    with jax.named_scope("hidden"):
        hidden, stats_mid, skipped = pl.pallas_call(
            functools.partial(
                hidden_kernel, float(rows * cols * (chans // GROUPS) * peers), peers
            ),
            out_shape=(
                whole((2 * rows + 2, 2, cols, outs), BF16),
                whole((peers, 8, LANES), F32),
                whole((rows * cols, outs), F32),
            ),
            in_specs=[taken, taken, far, taken, far, far, far, far],
            out_specs=(taken,) * 3,
            scratch_shapes=[
                VMEM(((rows + 2) * cols, chans), BF16),
                VMEM((9, (rows + 2) * cols, outs), F32),
                VMEM((2, 1, chans), F32),
                VMEM((rows, cols, chans), BF16),
                VMEM((9, chans, outs), BF16),
                VMEM((chans, outs), BF16),
                dma((13,)),
            ],
            compiler_params=params(24),
            name="hidden",
        )(
            stats,
            up,
            in_hbm(latent),
            down,
            in_hbm(gain_in.reshape(1, -1)),
            in_hbm(shift_in.reshape(1, -1)),
            in_hbm(conv_in),
            in_hbm(skip_weight),
        )
    with jax.named_scope("exchange_mid"):
        stats_mid = lax.all_to_all(stats_mid, axis, 0, 0)

    with jax.named_scope("output"):
        return pl.pallas_call(
            functools.partial(
                output_kernel, float(4 * rows * cols * (outs // GROUPS) * peers), peers
            ),
            out_shape=whole((2 * rows, 2 * cols, outs), BF16),
            in_specs=[taken, taken, far, far, far, taken],
            out_specs=far,
            scratch_shapes=[
                VMEM((2 * rows + 2, cols, 4 * outs), BF16),
                VMEM((outs // LANES, 2 * cols, LANES), F32),
                VMEM((2 * rows, 2 * cols, outs), BF16),
                VMEM(conv_mid.shape, BF16),
                VMEM((2, 1, outs), F32),
                dma((2 * rows,)),
                dma((3,)),
            ],
            compiler_params=params(24),
            name="output",
        )(
            stats_mid,
            hidden,
            in_hbm(gain_mid.reshape(1, -1)),
            in_hbm(shift_mid.reshape(1, -1)),
            in_hbm(conv_mid),
            skipped,
        )


def solution(mesh):
    placed = (P(("groups", "rows"), None, None), P(), P(), P(), P(), P(), P(), P())
    return jax.shard_map(
        body,
        mesh=mesh,
        in_specs=placed,
        out_specs=P(("groups", "rows"), None, None),
        check_vma=False,
    )
```

time: 44.2 us -> 45.1 us (1.020)
  blocking collectives: 0 us -> 25.4 us
  starting transfers between devices: 16.5 us -> 3.7 us
  Pallas kernels: 21.8 us -> 15.6 us
  waiting for transfers between devices: 5.4 us -> 0.01 us
    all_to_all x0 -> x2, blocking collectives: none -> 25.4 us  [the longest x1 15.9 us: body(): stats = lax.all_to_all(stats, axis, 0, 0)]
    all_to_all x2 -> x0, starting transfers between devices: 12.8 us -> none  [the longest x1 9.26 us: body(): stats = lax.all_to_all(stats, axis, 0, 0)]
    pallas_call x2 -> x0, Pallas kernels: 8.29 us -> none  [the longest x1 5.01 us: body(): pl.pallas_call(border_kernel, out_shape=(whole((2, 2, cols, outs), BF16),...]
    all_to_all x2 -> x0, waiting for transfers between devices: 5.39 us -> none  [the longest x1 3.57 us: body(): stats = lax.all_to_all(stats, axis, 0, 0)]
    pallas_call x1, Pallas kernels: 6.9 us -> 8.95 us  [body(): pl.pallas_call(functools.partial(hidden_kernel, float(rows * cols * (chan...]
    pallas_call x1, Pallas kernels: 4.84 us -> 5.55 us  [body(): pl.pallas_call(functools.partial(output_kernel, float(4 * rows * cols * (...]
    pallas_call x1, Pallas kernels: 1.75 us -> 1.12 us  [body(): pl.pallas_call(stats_kernel, out_shape=(whole((peers, 8, LANES), F32), wh...]
  transfers between devices with their start and end apart: 4 -> 2, of which waited for: 2 -> 0; matrix products, arithmetic and copies ran while one was open for 0% -> 0% of each run, Pallas kernels for 19% -> 0%
where the time goes in v3:
time: 45.1 us; the launch traced here: 44.8 us
  blocking collectives  25.4 us (56%)
  Pallas kernels  15.6 us (35%)
  starting transfers between devices  3.7 us (8%)
    all_to_all x1, blocking collectives, body(): stats = lax.all_to_all(stats, axis, 0, 0)  15.9 us
    all_to_all x1, blocking collectives, body(): stats_mid = lax.all_to_all(stats_mid, axis, 0, 0)  9.48 us
    pallas_call x1, Pallas kernels, body(): pl.pallas_call(functools.partial(hidden_kernel, float(rows * cols * (chan...  8.95 us
    pallas_call x1, Pallas kernels, body(): pl.pallas_call(functools.partial(output_kernel, float(4 * rows * cols * (...  5.55 us
    ppermute x1, starting transfers between devices, body(): up = lax.ppermute(tail, axis, [(i, i + 1) for i in range(ends)])  2.41 us
    ppermute x1, starting transfers between devices, body(): down = lax.ppermute(head, axis, [(i + 1, i) for i in range(ends)])  1.29 us
    pallas_call x1, Pallas kernels, body(): pl.pallas_call(stats_kernel, out_shape=(whole((peers, 8, LANES), F32), wh...  1.12 us
  transfers between devices with their start and end apart: 2, of which 0 were waited for; matrix products, arithmetic and copies ran while one was open for 0% of the time, Pallas kernels for 0%

profile of v3, /device:TPU:0, one launch (start us, length us, event | category | flops | bytes accessed | tf_op | source)
XLA Modules:
  0.0 44.8 jit_solution(10450616252212193512)
XLA Ops:
  0.0 1.1 %stats.1 = (f32[16,8,128]{2,1,0:T(8,128)S(1)}, bf16[1,256,512]{2,1,0:T(8,128)(2,1)S(1)}, bf16[1,256,512]{2,1,0:T(8,128)(2,1)S(1)}) custom-call(bf16[2,256,512]{2,1,0:T(8,128)(2,1)} %latent_ref.3), custom_call_target="tpu_custom_call" | custom-call | tf_op jit(solution)/shard_map/stats/stats/pallas_call | solution.py:271
  1.1 2.4 %collective-permute-start = (bf16[1,256,512]{2,1,0:T(8,128)(2,1)S(1)}, bf16[1,256,512]{2,1,0:T(8,128)(2,1)S(1)}, u32[]{:S(2)}, u32[]{:S(2)}) collective-permute-start(bf16[1,256,512]{2,1,0:T(8,128)(2,1)S(1)} %get-tuple-element.12), channel_id=1, source_target_pairs={{0,1},{1,2},{2,3},{3,4},{4,5},{5,6},{6,7},{7,8},{8,9},{9,10},{10,1... | collective-permute-start | bytes 786440 | tf_op jit(solution)/shard_map/halo/ppermute | solution.py:287
  3.5 1.3 %collective-permute-start.1 = (bf16[1,256,512]{2,1,0:T(8,128)(2,1)S(1)}, bf16[1,256,512]{2,1,0:T(8,128)(2,1)S(1)}, u32[]{:S(2)}, u32[]{:S(2)}) collective-permute-start(bf16[1,256,512]{2,1,0:T(8,128)(2,1)S(1)} %get-tuple-element.13), channel_id=1, source_target_pairs={{1,0},{2,1},{3,2},{4,3},{5,4},{6,5},{7,6},{8,7},{9,8},{10,9},{11,1... | collective-permute-start | bytes 786440 | tf_op jit(solution)/shard_map/halo/ppermute | solution.py:288
  4.8 15.9 %all_to_all.10.stats_ref = f32[16,8,128]{2,1,0:T(8,128)S(1)} all-to-all(f32[16,8,128]{2,1,0:T(8,128)S(1)} %get-tuple-element.11), channel_id=1, replica_groups=mesh['groups'=2,'rows'=16] {'rows'}, dimensions={0} | all-to-all | bytes 131072 | tf_op jit(solution)/shard_map/exchange_in/all_to_all | solution.py:285
  20.8 0.0 collective-permute-done.up_ref
  20.8 0.0 collective-permute-done.1.down_ref
  20.8 9.0 %hidden.1 = (bf16[6,2,256,256]{3,2,1,0:T(8,128)(2,1)S(1)}, f32[16,8,128]{2,1,0:T(8,128)S(1)}, f32[512,256]{1,0:T(8,128)S(1)}) custom-call(f32[16,8,128]{2,1,0:T(8,128)S(1)} %all_to_all.10.stats_ref, bf16[1,256,512]{2,1,0:T(8,128)(2,1)S(1)} %collective-permute-done.up_ref, bf16[2,256,512]{2,1,0:T(8,128)(2,1)} %latent_ref.3, ...), custom_call_target="tpu_custom_call" | custom-call | tf_op jit(solution)/shard_map/hidden/hidden/pallas_call | solution.py:291
  29.8 9.5 %all_to_all.11.stats_ref = f32[16,8,128]{2,1,0:T(8,128)S(1)} all-to-all(f32[16,8,128]{2,1,0:T(8,128)S(1)} %get-tuple-element.14), channel_id=1, replica_groups=mesh['groups'=2,'rows'=16] {'rows'}, dimensions={0} | all-to-all | bytes 131072 | tf_op jit(solution)/shard_map/exchange_mid/all_to_all | solution.py:324
  39.2 5.5 %output.1 = bf16[4,512,256]{2,1,0:T(8,128)(2,1)} custom-call(f32[16,8,128]{2,1,0:T(8,128)S(1)} %all_to_all.11.stats_ref, bf16[6,2,256,256]{3,2,1,0:T(8,128)(2,1)S(1)} %get-tuple-element.15.hidden_ref, f32[1,256]{1,0:T(1,128)} %bitcast.6, f32[1,256]{1,0:T(1,128)} %bitcast.7, bf16[2304,256]{1,0:T(8,128)(2,1)} %weight_ref.3, ...), custom_call_target="tpu_custom_call" | custom-call | tf_op jit(solution)/shard_map/output/output/pallas_call | solution.py:327
Async XLA Ops:
  1.1 19.7 %collective-permute-start = (bf16[1,256,512]{2,1,0:T(8,128)(2,1)S(1)}, bf16[1,256,512]{2,1,0:T(8,128)(2,1)S(1)}, u32[]{:S(2)}, u32[]{:S(2)}) collective-permute-start(bf16[1,256,512]{2,1,0:T(8,128)(2,1)S(1)} %get-tuple-element.12), channel_id=1, source_target_pairs={{0,1},{1,2},{2,3},{3,4},{4,5},{5,6},{6,7},{7,8},{8,9},{9,10},{10,1... | collective-permute-start | bytes 786440 | tf_op jit(solution)/shard_map/halo/ppermute | solution.py:287
  3.5 17.2 %collective-permute-start.1 = (bf16[1,256,512]{2,1,0:T(8,128)(2,1)S(1)}, bf16[1,256,512]{2,1,0:T(8,128)(2,1)S(1)}, u32[]{:S(2)}, u32[]{:S(2)}) collective-permute-start(bf16[1,256,512]{2,1,0:T(8,128)(2,1)S(1)} %get-tuple-element.13), channel_id=1, source_target_pairs={{1,0},{2,1},{3,2},{4,3},{5,4},{6,5},{7,6},{8,7},{9,8},{10,9},{11,1... | collective-permute-start | bytes 786440 | tf_op jit(solution)/shard_map/halo/ppermute | solution.py:288

commit v4 on v3

v4 whole, which is shorter than its diff:
```python
import functools

import jax
import jax.numpy as jnp
from jax import lax
from jax.experimental import pallas as pl
from jax.experimental.pallas import tpu as pltpu
from jax.sharding import PartitionSpec as P

GROUPS = 32
EPS = 1e-06
F32 = jnp.float32
BF16 = jnp.bfloat16
LANES = 128
GUARD = 8
SPLIT = 2
EARLY = 3
STEP = 16
VMEM = pltpu.VMEM


def vmem_spec():
    return pl.BlockSpec(memory_space=VMEM)


def in_hbm(values):
    return pltpu.with_memory_space_constraint(values, pltpu.HBM)


def params(limit_mib):
    return pltpu.CompilerParams(vmem_limit_bytes=limit_mib << 20)


def cost(flops, data):
    return pl.CostEstimate(flops=flops, bytes_accessed=data, transcendentals=0)


def stack_lanes(row):
    count = row.shape[1] // LANES
    return [row[:, i * LANES : (i + 1) * LANES] for i in range(count)]


def put_stats(out_ref, total, square):
    rows = stack_lanes(total) + stack_lanes(square)
    fill = 8 - len(rows)
    if fill:
        rows.append(jnp.zeros((fill, LANES), F32))
    tile = jnp.concatenate(rows, axis=0)
    out_ref[...] = jnp.broadcast_to(tile[None], out_ref.shape)


def get_affine(stats_ref, gain, shift, group_width, count):
    chans = gain.shape[1]
    half = chans // LANES
    total = jnp.sum(stats_ref[...], axis=0)
    left = lax.broadcasted_iota(jnp.int32, (LANES, LANES), 0) // group_width
    right = lax.broadcasted_iota(jnp.int32, (LANES, LANES), 1) // group_width
    same = (left == right).astype(F32)
    pooled = jnp.dot(total, same, preferred_element_type=F32, precision=lax.Precision.HIGHEST)
    scaled = pooled * (1.0 / count)
    center = jnp.concatenate([scaled[i : i + 1] for i in range(half)], axis=1)
    moment = jnp.concatenate([scaled[half + i : half + i + 1] for i in range(half)], axis=1)
    spread = jnp.maximum(moment - center * center, 0.0)
    scale = gain * lax.rsqrt(spread + EPS)
    return 0.5 * scale, 0.5 * (shift - center * scale)


def half_silu(values, scale, offset):
    halved = values * scale + offset
    return halved + halved * jnp.tanh(halved)


def shift_rows(values, step):
    size = values.shape[0]
    moved = pltpu.roll(values, step % size, 0)
    place = lax.broadcasted_iota(jnp.int32, (size, 1), 0)
    edge = 0 if step == 1 else size - 1
    return jnp.where(place == edge, 0.0, moved)


def stats_kernel(latent_ref, stats_ref, head_ref, tail_ref, held_ref, sems):
    rows = latent_ref.shape[0]
    copies = [
        pltpu.make_async_copy(latent_ref.at[row], held_ref.at[row], sems.at[row])
        for row in range(rows)
    ]
    for copy in copies:
        copy.start()
    total, square = 0.0, 0.0
    for row in range(rows):
        copies[row].wait()
        values = held_ref[row].astype(F32)
        total += jnp.sum(values, axis=0, keepdims=True)
        square += jnp.sum(values * values, axis=0, keepdims=True)
    put_stats(stats_ref, total, square)
    head_ref[0] = held_ref[0]
    tail_ref[0] = held_ref[rows - 1]


def fetch_all(pairs, sems):
    copies = [
        pltpu.make_async_copy(source, target, sems.at[index])
        for index, (source, target) in enumerate(pairs)
    ]
    for copy in copies:
        copy.start()
    return copies


def load_kernel(*refs):
    count = len(refs) // 2
    pairs = [
        (source.at[pl.ds(0, target.shape[0]), :], target)
        for source, target in zip(refs[:count], refs[count : 2 * count])
    ]
    for copy in fetch_all(pairs, refs[-1]):
        copy.wait()


def hidden_kernel(
    count,
    axis_count,
    stats_ref,
    up_ref,
    latent_ref,
    down_ref,
    gain_ref,
    shift_ref,
    weight_ref,
    rest_ref,
    hidden_ref,
    out_ref,
    middle_ref,
    act_ref,
    tap_ref,
    near_ref,
    late_ref,
    sems,
):
    rows, cols, chans = latent_ref.shape
    outs = weight_ref.shape[1]
    split = EARLY * chans
    fetched, fetched_late = fetch_all(
        [(latent_ref, near_ref), (rest_ref.at[pl.ds(split, (9 - EARLY) * chans), :], late_ref)],
        sems,
    )
    halves = outs // LANES
    pitch = cols + GUARD
    part = cols // SPLIT
    scale, offset = get_affine(stats_ref, gain_ref[...], shift_ref[...], chans // GROUPS, count)
    place = lax.axis_index("rows")
    total_rows = 2 * rows + 2
    sources = [[(row + tap - 2) // 2 + 1 for tap in range(3)] for row in range(total_rows)]
    zeros = jnp.zeros((GUARD, LANES), F32)
    for tap in range(9):
        if tap % 3 != 1:
            for row in range(rows + 3):
                for half in range(halves):
                    tap_ref[tap, half, row * pitch : row * pitch + GUARD, :] = zeros

    def fill(piece, wanted):
        span = slice(piece * part, (piece + 1) * part)
        for row in wanted:
            keep = None
            if row == 0:
                source, keep = up_ref[0, span], place > 0
            elif row == rows + 1:
                source, keep = down_ref[0, span], place < axis_count - 1
            else:
                source = near_ref[row - 1, span]
            act = half_silu(source.astype(F32), scale, offset)
            if keep is not None:
                act = act * keep.astype(F32)
            act_ref[row, span, :] = act.astype(BF16)

    def multiply(piece, taps):
        span = slice(piece * part, (piece + 1) * part)
        for tap in taps:
            if tap < EARLY:
                weight = weight_ref[tap * chans : (tap + 1) * chans, :]
            else:
                weight = late_ref[(tap - EARLY) * chans : (tap + 1 - EARLY) * chans, :]
            used = [source[tap // 3] for source in sources]
            first, last = min(used), max(used) + 1
            found = jnp.dot(
                act_ref[first:last, span, :].reshape(-1, chans),
                weight,
                preferred_element_type=F32,
            )
            for row in range(first, last):
                start = row * pitch + GUARD + piece * part
                for half in range(halves):
                    tap_ref[tap, half, start : start + part, :] = found[
                        (row - first) * part : (row - first + 1) * part,
                        half * LANES : (half + 1) * LANES,
                    ]

    totals = [jnp.zeros((8, LANES), F32)] * halves
    squares = [jnp.zeros((8, LANES), F32)] * halves

    def combine(chunk):
        for half in range(halves):
            sums = {}
            for row, tap in sorted({(s[a], a) for s in sources for a in range(3)}):
                start = row * pitch + GUARD + chunk * STEP

                def get(b, move):
                    return tap_ref[3 * tap + b, half, start + move : start + move + STEP, :]

                left, center, right = get(0, 0), get(1, 0), get(2, 0)
                sums[row, tap] = (
                    get(0, -1) + (center + right),
                    (left + center) + get(2, 1),
                )
            for row in range(total_rows):
                for phase in range(2):
                    pieces = [sums[sources[row][a], a][phase] for a in range(3)]
                    found = (pieces[0] + pieces[1] + pieces[2]).astype(BF16)
                    hidden_ref[
                        row,
                        phase,
                        chunk * STEP : (chunk + 1) * STEP,
                        half * LANES : (half + 1) * LANES,
                    ] = found
                    if 0 < row < total_rows - 1:
                        wide = found.astype(F32)
                        upper, lower = wide[:8], wide[8:]
                        totals[half] = totals[half] + (upper + lower)
                        squares[half] = squares[half] + (upper * upper + lower * lower)

    chunks = cols // STEP
    ready = [(piece + 1) * part // STEP - 1 for piece in range(SPLIT)]
    ready[-1] = chunks
    for piece in range(SPLIT):
        fill(piece, (0, rows + 1))
    fetched.wait()
    for piece in range(SPLIT):
        fill(piece, range(1, rows + 1))
        multiply(piece, range(EARLY))
    middle_ref[...] = act_ref[1 : rows + 1].reshape(-1, chans)
    fetched_late.wait()
    for piece in range(SPLIT):
        multiply(piece, range(EARLY, 9))
    done = 0
    for piece in range(SPLIT):
        for chunk in range(done, ready[piece]):
            combine(chunk)
        done = ready[piece]
    put_stats(
        out_ref,
        jnp.concatenate([jnp.sum(t, axis=0, keepdims=True) for t in totals], axis=1),
        jnp.concatenate([jnp.sum(t, axis=0, keepdims=True) for t in squares], axis=1),
    )


def skip_kernel(
    middle_ref,
    skip_ref,
    gain_ref,
    shift_ref,
    skipped_ref,
    gain_out_ref,
    shift_out_ref,
    held_ref,
    sems,
):
    copies = fetch_all(
        [
            (skip_ref, held_ref),
            (gain_ref, gain_out_ref),
            (shift_ref, shift_out_ref),
        ],
        sems,
    )
    for copy in copies:
        copy.wait()
    skipped_ref[...] = jnp.dot(middle_ref[...], held_ref[...], preferred_element_type=F32)


def output_kernel(
    count,
    axis_count,
    stats_ref,
    hidden_ref,
    gain_ref,
    shift_ref,
    weight_ref,
    skipped_ref,
    out_ref,
    mid_ref,
    mixed_ref,
    done_ref,
    held_ref,
    sems,
    held_sem,
):
    fetched = pltpu.make_async_copy(weight_ref, held_ref, held_sem)
    fetched.start()
    total_rows, _, cols, chans = hidden_ref.shape
    rows = total_rows - 2
    scale, offset = get_affine(stats_ref, gain_ref[...], shift_ref[...], chans // GROUPS, count)
    place = lax.axis_index("rows")

    def fill(row):
        pair = []
        keep = None
        if row == 0:
            keep = place > 0
        elif row == rows + 1:
            keep = place < axis_count - 1
        for phase in range(2):
            value = half_silu(hidden_ref[row, phase].astype(F32), scale, offset)
            if keep is not None:
                value = value * keep.astype(F32)
            pair.append(value)
        even, odd = pair
        mid_ref[row, :, 0:chans] = shift_rows(odd, 1).astype(BF16)
        mid_ref[row, :, chans : 2 * chans] = even.astype(BF16)
        mid_ref[row, :, 2 * chans : 3 * chans] = odd.astype(BF16)
        mid_ref[row, :, 3 * chans :] = shift_rows(even, -1).astype(BF16)

    def multiply(low):
        lhs = jnp.concatenate(
            [
                jnp.concatenate(
                    [
                        mid_ref[2 * low + tap : 2 * low + tap + 2, :, window].reshape(
                            -1, 3 * chans
                        )
                        for tap in range(3)
                    ],
                    axis=1,
                )
                for window in (slice(0, 3 * chans), slice(chans, 4 * chans))
            ],
            axis=0,
        )
        return jnp.dot(lhs, held_ref[...], preferred_element_type=F32)

    def finish(low, found):
        base = skipped_ref[low * cols : (low + 1) * cols, :]
        for side in range(2):
            row = 2 * low + side
            for phase in range(2):
                start = (2 * phase + side) * cols
                value = base + found[start : start + cols]
                for half in range(chans // LANES):
                    mixed_ref[row, half, pl.ds(phase, cols, stride=2), :] = value[
                        :, half * LANES : (half + 1) * LANES
                    ]
            for half in range(chans // LANES):
                done_ref[row, :, half * LANES : (half + 1) * LANES] = mixed_ref[row, half].astype(
                    BF16
                )

    found = []
    filled = 0
    for low in range(rows // 2):
        for row in range(filled, 2 * low + 4):
            fill(row)
        filled = 2 * low + 4
        if low == 0:
            fetched.wait()
        found.append(multiply(low))
    copies = []
    for low in range(rows // 2):
        finish(low, found[low])
        for row in (2 * low, 2 * low + 1):
            copies.append(pltpu.make_async_copy(done_ref.at[row], out_ref.at[row], sems.at[row]))
            copies[-1].start()
    for copy in copies:
        copy.wait()


def body(latent, gain_in, shift_in, conv_in, gain_mid, shift_mid, conv_mid, skip_weight):
    axis = "rows"
    peers = lax.axis_size(axis)
    rows, cols, chans = latent.shape
    outs = conv_in.shape[1]
    ends = peers - 1
    taken = vmem_spec()
    far = pl.BlockSpec(memory_space=pltpu.HBM)
    dma = pltpu.SemaphoreType.DMA
    whole = jax.ShapeDtypeStruct

    with jax.named_scope("stats"):
        stats, head, tail = pl.pallas_call(
            stats_kernel,
            out_shape=(
                whole((peers, 8, LANES), F32),
                whole((1, cols, chans), BF16),
                whole((1, cols, chans), BF16),
            ),
            in_specs=[far],
            out_specs=(taken,) * 3,
            scratch_shapes=[VMEM(latent.shape, BF16), dma((rows,))],
            compiler_params=params(16),
            name="stats",
        )(in_hbm(latent))
    with jax.named_scope("exchange_in"):
        stats = lax.all_to_all(stats, axis, 0, 0)
    with jax.named_scope("halo"):
        up = lax.ppermute(tail, axis, [(i, i + 1) for i in range(ends)])
        down = lax.ppermute(head, axis, [(i + 1, i) for i in range(ends)])

    with jax.named_scope("load"):
        ready = [gain_in.reshape(1, -1), shift_in.reshape(1, -1), conv_in]
        ready = pl.pallas_call(
            load_kernel,
            out_shape=[
                VMEM((1, chans), F32),
                VMEM((1, chans), F32),
                VMEM((EARLY * chans, outs), BF16),
            ],
            in_specs=[far] * 3,
            out_specs=[taken] * 3,
            scratch_shapes=[dma((3,))],
            compiler_params=params(4),
            cost_estimate=cost(4 << 20, 8 << 20),
            name="load",
        )(*map(in_hbm, ready))
        near_gain, near_shift, near_conv = ready

    with jax.named_scope("hidden"):
        hidden, stats_mid, middle = pl.pallas_call(
            functools.partial(
                hidden_kernel, float(rows * cols * (chans // GROUPS) * peers), peers
            ),
            out_shape=(
                whole((2 * rows + 2, 2, cols, outs), BF16),
                whole((peers, 8, LANES), F32),
                whole((rows * cols, chans), BF16),
            ),
            in_specs=[taken, taken, far, taken, taken, taken, taken, far],
            out_specs=(taken,) * 3,
            scratch_shapes=[
                VMEM((rows + 2, cols, chans), BF16),
                VMEM((9, outs // LANES, (rows + 2) * (cols + GUARD) + GUARD, LANES), F32),
                VMEM(latent.shape, BF16),
                VMEM(((9 - EARLY) * chans, outs), BF16),
                dma((2,)),
            ],
            compiler_params=params(24),
            name="hidden",
        )(stats, up, in_hbm(latent), down, near_gain, near_shift, near_conv, in_hbm(conv_in))
    with jax.named_scope("exchange_mid"):
        stats_mid = lax.all_to_all(stats_mid, axis, 0, 0)

    with jax.named_scope("skip"):
        skipped, near_gain, near_shift = pl.pallas_call(
            skip_kernel,
            out_shape=[
                VMEM((rows * cols, outs), F32),
                VMEM((1, outs), F32),
                VMEM((1, outs), F32),
            ],
            in_specs=[taken] + [far] * 3,
            out_specs=[taken] * 3,
            scratch_shapes=[VMEM((chans, outs), BF16), dma((3,))],
            compiler_params=params(4),
            cost_estimate=cost(200 << 20, 8 << 20),
            name="skip",
        )(
            middle,
            in_hbm(skip_weight),
            in_hbm(gain_mid.reshape(1, -1)),
            in_hbm(shift_mid.reshape(1, -1)),
        )

    with jax.named_scope("output"):
        return pl.pallas_call(
            functools.partial(
                output_kernel, float(4 * rows * cols * (outs // GROUPS) * peers), peers
            ),
            out_shape=whole((2 * rows, 2 * cols, outs), BF16),
            in_specs=[taken] * 4 + [far, taken],
            out_specs=far,
            scratch_shapes=[
                VMEM((2 * rows + 2, cols, 4 * outs), BF16),
                VMEM((2 * rows, outs // LANES, 2 * cols, LANES), F32),
                VMEM((2 * rows, 2 * cols, outs), BF16),
                VMEM(conv_mid.shape, BF16),
                dma((2 * rows,)),
                dma,
            ],
            compiler_params=params(24),
            name="output",
        )(stats_mid, hidden, near_gain, near_shift, in_hbm(conv_mid), skipped)


def solution(mesh):
    placed = (P(("groups", "rows"), None, None), P(), P(), P(), P(), P(), P(), P())
    return jax.shard_map(
        body,
        mesh=mesh,
        in_specs=placed,
        out_specs=P(("groups", "rows"), None, None),
        check_vma=False,
    )
```

time: 45.1 us -> 42.9 us (0.951)
  blocking collectives: 25.4 us -> 0 us
  starting transfers between devices: 3.7 us -> 16.5 us
  waiting for transfers between devices: 0.01 us -> 11.3 us
  Pallas kernels: 15.6 us -> 14.7 us
    all_to_all x2 -> x0, blocking collectives: 25.4 us -> none  [the longest x1 15.9 us: body(): stats = lax.all_to_all(stats, axis, 0, 0)]
    all_to_all x0 -> x2, starting transfers between devices: none -> 12.8 us  [the longest x1 9.26 us: body(): stats = lax.all_to_all(stats, axis, 0, 0)]
    all_to_all x0 -> x2, waiting for transfers between devices: none -> 11.3 us  [the longest x1 5.69 us: body(): stats = lax.all_to_all(stats, axis, 0, 0)]
    pallas_call x1, Pallas kernels: 8.95 us -> 5.25 us  [body(): pl.pallas_call(functools.partial(hidden_kernel, float(rows * cols * (chan...]
    pallas_call x0 -> x2, Pallas kernels: none -> 2.48 us  [the longest x1 1.28 us: body(): pl.pallas_call(skip_kernel, out_shape=[VMEM((rows * cols, outs), F32), VM...]
    pallas_call x1, Pallas kernels: 1.12 us -> 1.75 us  [body(): pl.pallas_call(stats_kernel, out_shape=(whole((peers, 8, LANES), F32), wh...]
  transfers between devices with their start and end apart: 2 -> 4, of which waited for: 0 -> 2; matrix products, arithmetic and copies ran while one was open for 0% -> 0% of each run, Pallas kernels for 0% -> 6%
where the time goes in v4:
time: 42.9 us; the launch traced here: 42.5 us
  starting transfers between devices  16.5 us (38%)
  Pallas kernels  14.7 us (34%)
  waiting for transfers between devices  11.3 us (26%)
    all_to_all x1, starting transfers between devices, body(): stats = lax.all_to_all(stats, axis, 0, 0)  9.26 us
    all_to_all x1, waiting for transfers between devices, body(): stats = lax.all_to_all(stats, axis, 0, 0)  5.69 us
    all_to_all x1, waiting for transfers between devices, body(): stats_mid = lax.all_to_all(stats_mid, axis, 0, 0)  5.57 us
    pallas_call x1, Pallas kernels, body(): pl.pallas_call(functools.partial(hidden_kernel, float(rows * cols * (chan...  5.25 us
    pallas_call x1, Pallas kernels, body(): pl.pallas_call(functools.partial(output_kernel, float(4 * rows * cols * (...  5.21 us
    all_to_all x1, starting transfers between devices, body(): stats_mid = lax.all_to_all(stats_mid, axis, 0, 0)  3.51 us
    ppermute x1, starting transfers between devices, body(): up = lax.ppermute(tail, axis, [(i, i + 1) for i in range(ends)])  2.41 us
    pallas_call x1, Pallas kernels, body(): pl.pallas_call(stats_kernel, out_shape=(whole((peers, 8, LANES), F32), wh...  1.75 us
  transfers between devices with their start and end apart: 4, of which 2 were waited for; matrix products, arithmetic and copies ran while one was open for 0% of the time, Pallas kernels for 6%

profile of v4, /device:TPU:0, one launch (start us, length us, event | category | flops | bytes accessed | tf_op | source)
XLA Modules:
  0.0 42.5 jit_solution(11103015727672061375)
XLA Ops:
  0.0 1.7 %stats.1 = (f32[16,8,128]{2,1,0:T(8,128)}, bf16[1,256,512]{2,1,0:T(8,128)(2,1)S(1)}, bf16[1,256,512]{2,1,0:T(8,128)(2,1)S(1)}) custom-call(bf16[2,256,512]{2,1,0:T(8,128)(2,1)} %latent_ref.3), custom_call_target="tpu_custom_call" | custom-call | tf_op jit(solution)/shard_map/stats/stats/pallas_call | solution.py:387
  1.8 2.4 %collective-permute-start = (bf16[1,256,512]{2,1,0:T(8,128)(2,1)S(1)}, bf16[1,256,512]{2,1,0:T(8,128)(2,1)S(1)}, u32[]{:S(2)}, u32[]{:S(2)}) collective-permute-start(bf16[1,256,512]{2,1,0:T(8,128)(2,1)S(1)} %get-tuple-element.18), channel_id=1, source_target_pairs={{0,1},{1,2},{2,3},{3,4},{4,5},{5,6},{6,7},{7,8},{8,9},{9,10},{10,1... | collective-permute-start | bytes 786440 | tf_op jit(solution)/shard_map/halo/ppermute | solution.py:403
  4.2 1.3 %collective-permute-start.1 = (bf16[1,256,512]{2,1,0:T(8,128)(2,1)S(1)}, bf16[1,256,512]{2,1,0:T(8,128)(2,1)S(1)}, u32[]{:S(2)}, u32[]{:S(2)}) collective-permute-start(bf16[1,256,512]{2,1,0:T(8,128)(2,1)S(1)} %get-tuple-element.19), channel_id=1, source_target_pairs={{1,0},{2,1},{3,2},{4,3},{5,4},{6,5},{7,6},{8,7},{9,8},{10,9},{11,1... | collective-permute-start | bytes 786440 | tf_op jit(solution)/shard_map/halo/ppermute | solution.py:404
  5.5 9.3 %all-to-all-start = ((f32[16,8,128]{2,1,0:T(8,128)}), f32[16,8,128]{2,1,0:T(8,128)S(1)}, u32[]{:S(2)}, u32[]{:S(2)}) async-start(f32[16,8,128]{2,1,0:T(8,128)} %get-tuple-element.17), calls=%async_computation | async-start | bytes 131072 | tf_op jit(solution)/shard_map/exchange_in/all_to_all | solution.py:401
  14.7 1.2 %load.1 = (f32[1,512]{1,0:T(1,128)S(1)}, f32[1,512]{1,0:T(1,128)S(1)}, bf16[1536,256]{1,0:T(8,128)(2,1)S(1)}) custom-call(f32[1,512]{1,0:T(1,128)} %bitcast.4, f32[1,512]{1,0:T(1,128)} %bitcast.5, bf16[4608,256]{1,0:T(8,128)(2,1)} %rest_ref.1), custom_call_target="tpu_custom_call" | custom-call | flops 4194304 | bytes 8388608 | tf_op jit(solution)/shard_map/load/load/pallas_call | solution.py:408
  15.9 5.7 %all-to-all-done.stats_ref = f32[16,8,128]{2,1,0:T(8,128)S(1)} async-done(((f32[16,8,128]{2,1,0:T(8,128)}), f32[16,8,128]{2,1,0:T(8,128)S(1)}, u32[]{:S(2)}, u32[]{:S(2)}) %all-to-all-start) | async-done | bytes 65568 | tf_op jit(solution)/shard_map/exchange_in/all_to_all | solution.py:401
  21.6 0.0 collective-permute-done.up_ref
  21.6 0.0 collective-permute-done.1.down_ref
  21.6 5.3 %hidden.1 = (bf16[6,2,256,256]{3,2,1,0:T(8,128)(2,1)S(1)}, f32[16,8,128]{2,1,0:T(8,128)}, bf16[512,512]{1,0:T(8,128)(2,1)S(1)}) custom-call(f32[16,8,128]{2,1,0:T(8,128)S(1)} %all-to-all-done.stats_ref, bf16[1,256,512]{2,1,0:T(8,128)(2,1)S(1)} %collective-permute-done.up_ref, bf16[2,256,512]{2,1,0:T(8,128)(2,1)} %latent_ref.3, ...), custom_call_target="tpu_custom_call" | custom-call | tf_op jit(solution)/shard_map/hidden/hidden/pallas_call | solution.py:425
  26.9 3.5 %all-to-all-start.1 = ((f32[16,8,128]{2,1,0:T(8,128)}), f32[16,8,128]{2,1,0:T(8,128)S(1)}, u32[]{:S(2)}, u32[]{:S(2)}) async-start(f32[16,8,128]{2,1,0:T(8,128)} %get-tuple-element.23), calls=%async_computation.1 | async-start | bytes 131072 | tf_op jit(solution)/shard_map/exchange_mid/all_to_all | solution.py:447
  30.4 1.3 %skip.1 = (f32[512,256]{1,0:T(8,128)S(1)}, f32[1,256]{1,0:T(1,128)S(1)}, f32[1,256]{1,0:T(1,128)S(1)}) custom-call(bf16[512,512]{1,0:T(8,128)(2,1)S(1)} %get-tuple-element.25.middle_ref, bf16[512,256]{1,0:T(8,128)(2,1)} %skip_ref.1, f32[1,256]{1,0:T(1,128)} %bitcast.6, f32[1,256]{1,0:T(1,128)} %bitcast.7), custom_call_target="tpu_custom_call" | custom-call | flops 209715200 | bytes 8388608 | tf_op jit(solution)/shard_map/skip/skip/pallas_call | solution.py:450
  31.7 5.6 %all-to-all-done.1.stats_ref = f32[16,8,128]{2,1,0:T(8,128)S(1)} async-done(((f32[16,8,128]{2,1,0:T(8,128)}), f32[16,8,128]{2,1,0:T(8,128)S(1)}, u32[]{:S(2)}, u32[]{:S(2)}) %all-to-all-start.1) | async-done | bytes 65568 | tf_op jit(solution)/shard_map/exchange_mid/all_to_all | solution.py:447
  37.3 5.2 %output.1 = bf16[4,512,256]{2,1,0:T(8,128)(2,1)} custom-call(f32[16,8,128]{2,1,0:T(8,128)S(1)} %all-to-all-done.1.stats_ref, bf16[6,2,256,256]{3,2,1,0:T(8,128)(2,1)S(1)} %get-tuple-element.24.hidden_ref, f32[1,256]{1,0:T(1,128)S(1)} %get-tuple-element.26.gain_ref, f32[1,256]{1,0:T(1,128)S(1)} %get-tuple-element.27.shift_ref, bf16[2304,256]{1,0:T(8,128)(2,1)} %weight_ref.1, ...), custom_call_target="tpu_custom_call" | custom-call | tf_op jit(solution)/shard_map/output/output/pallas_call | solution.py:471
Async XLA Ops:
  1.8 19.9 %collective-permute-start = (bf16[1,256,512]{2,1,0:T(8,128)(2,1)S(1)}, bf16[1,256,512]{2,1,0:T(8,128)(2,1)S(1)}, u32[]{:S(2)}, u32[]{:S(2)}) collective-permute-start(bf16[1,256,512]{2,1,0:T(8,128)(2,1)S(1)} %get-tuple-element.18), channel_id=1, source_target_pairs={{0,1},{1,2},{2,3},{3,4},{4,5},{5,6},{6,7},{7,8},{8,9},{9,10},{10,1... | collective-permute-start | bytes 786440 | tf_op jit(solution)/shard_map/halo/ppermute | solution.py:403
  4.2 17.5 %collective-permute-start.1 = (bf16[1,256,512]{2,1,0:T(8,128)(2,1)S(1)}, bf16[1,256,512]{2,1,0:T(8,128)(2,1)S(1)}, u32[]{:S(2)}, u32[]{:S(2)}) collective-permute-start(bf16[1,256,512]{2,1,0:T(8,128)(2,1)S(1)} %get-tuple-element.19), channel_id=1, source_target_pairs={{1,0},{2,1},{3,2},{4,3},{5,4},{6,5},{7,6},{8,7},{9,8},{10,9},{11,1... | collective-permute-start | bytes 786440 | tf_op jit(solution)/shard_map/halo/ppermute | solution.py:404
  5.5 16.2 %all-to-all-start = ((f32[16,8,128]{2,1,0:T(8,128)}), f32[16,8,128]{2,1,0:T(8,128)S(1)}, u32[]{:S(2)}, u32[]{:S(2)}) async-start(f32[16,8,128]{2,1,0:T(8,128)} %get-tuple-element.17), calls=%async_computation | async-start | bytes 131072 | tf_op jit(solution)/shard_map/exchange_in/all_to_all | solution.py:401
  26.9 10.4 %all-to-all-start.1 = ((f32[16,8,128]{2,1,0:T(8,128)}), f32[16,8,128]{2,1,0:T(8,128)S(1)}, u32[]{:S(2)}, u32[]{:S(2)}) async-start(f32[16,8,128]{2,1,0:T(8,128)} %get-tuple-element.23), calls=%async_computation.1 | async-start | bytes 131072 | tf_op jit(solution)/shard_map/exchange_mid/all_to_all | solution.py:447

commit v5 on v4

--- a/solution.py
+++ b/solution.py
@@ -6,6 +6,7 @@
 from jax.experimental import pallas as pl
 from jax.experimental.pallas import tpu as pltpu
 from jax.sharding import PartitionSpec as P
+
 
 GROUPS = 32
 EPS = 1e-06
@@ -14,7 +15,7 @@
 LANES = 128
 GUARD = 8
 SPLIT = 2
-EARLY = 3
+EARLY = 1
 STEP = 16
 VMEM = pltpu.VMEM
 
@@ -78,7 +79,7 @@
     return jnp.where(place == edge, 0.0, moved)
 
 
-def stats_kernel(latent_ref, stats_ref, head_ref, tail_ref, held_ref, sems):
+def stats_kernel(latent_ref, stats_ref, near_ref, far_ref, held_ref, sems):
     rows = latent_ref.shape[0]
     copies = [
         pltpu.make_async_copy(latent_ref.at[row], held_ref.at[row], sems.at[row])
@@ -93,8 +94,9 @@
         total += jnp.sum(values, axis=0, keepdims=True)
         square += jnp.sum(values * values, axis=0, keepdims=True)
     put_stats(stats_ref, total, square)
-    head_ref[0] = held_ref[0]
-    tail_ref[0] = held_ref[rows - 1]
+    odd = lax.rem(lax.axis_index("rows"), 2)
+    near_ref[0] = held_ref[(1 - odd) * (rows - 1)]
+    far_ref[0] = held_ref[odd * (rows - 1)]
 
 
 def fetch_all(pairs, sems):
@@ -110,7 +112,7 @@
 def load_kernel(*refs):
     count = len(refs) // 2
     pairs = [
-        (source.at[pl.ds(0, target.shape[0]), :], target)
+        (source.at[pl.ds(0, target.shape[0])], target)
         for source, target in zip(refs[:count], refs[count : 2 * count])
     ]
     for copy in fetch_all(pairs, refs[-1]):
@@ -121,27 +123,28 @@
     count,
     axis_count,
     stats_ref,
-    up_ref,
+    near_row_ref,
+    far_row_ref,
     latent_ref,
-    down_ref,
     gain_ref,
     shift_ref,
     weight_ref,
     rest_ref,
+    skip_ref,
     hidden_ref,
     out_ref,
-    middle_ref,
+    skipped_ref,
     act_ref,
     tap_ref,
-    near_ref,
     late_ref,
+    skips_ref,
     sems,
 ):
     rows, cols, chans = latent_ref.shape
     outs = weight_ref.shape[1]
     split = EARLY * chans
-    fetched, fetched_late = fetch_all(
-        [(latent_ref, near_ref), (rest_ref.at[pl.ds(split, (9 - EARLY) * chans), :], late_ref)],
+    fetched = fetch_all(
+        [(rest_ref.at[pl.ds(split, (9 - EARLY) * chans), :], late_ref), (skip_ref, skips_ref)],
         sems,
     )
     halves = outs // LANES
@@ -149,6 +152,7 @@
     part = cols // SPLIT
     scale, offset = get_affine(stats_ref, gain_ref[...], shift_ref[...], chans // GROUPS, count)
     place = lax.axis_index("rows")
+    odd = lax.rem(place, 2) == 1
     total_rows = 2 * rows + 2
     sources = [[(row + tap - 2) // 2 + 1 for tap in range(3)] for row in range(total_rows)]
     zeros = jnp.zeros((GUARD, LANES), F32)
@@ -163,12 +167,14 @@
         for row in wanted:
             keep = None
             if row == 0:
-                source, keep = up_ref[0, span], place > 0
+                keep = place > 0
+                source = jnp.where(odd, near_row_ref[0, span].astype(F32), far_row_ref[0, span].astype(F32))
             elif row == rows + 1:
-                source, keep = down_ref[0, span], place < axis_count - 1
+                keep = place < axis_count - 1
+                source = jnp.where(odd, far_row_ref[0, span].astype(F32), near_row_ref[0, span].astype(F32))
             else:
-                source = near_ref[row - 1, span]
-            act = half_silu(source.astype(F32), scale, offset)
+                source = latent_ref[row - 1, span].astype(F32)
+            act = half_silu(source, scale, offset)
             if keep is not None:
                 act = act * keep.astype(F32)
             act_ref[row, span, :] = act.astype(BF16)
@@ -232,15 +238,15 @@
     ready = [(piece + 1) * part // STEP - 1 for piece in range(SPLIT)]
     ready[-1] = chunks
     for piece in range(SPLIT):
-        fill(piece, (0, rows + 1))
-    fetched.wait()
-    for piece in range(SPLIT):
-        fill(piece, range(1, rows + 1))
+        fill(piece, range(rows + 2))
         multiply(piece, range(EARLY))
-    middle_ref[...] = act_ref[1 : rows + 1].reshape(-1, chans)
-    fetched_late.wait()
+    for copy in fetched:
+        copy.wait()
     for piece in range(SPLIT):
         multiply(piece, range(EARLY, 9))
+    skipped_ref[...] = jnp.dot(
+        act_ref[1 : rows + 1].reshape(-1, chans), skips_ref[...], preferred_element_type=F32
+    )
     done = 0
     for piece in range(SPLIT):
         for chunk in range(done, ready[piece]):
@@ -251,30 +257,6 @@
         jnp.concatenate([jnp.sum(t, axis=0, keepdims=True) for t in totals], axis=1),
         jnp.concatenate([jnp.sum(t, axis=0, keepdims=True) for t in squares], axis=1),
     )
-
-
-def skip_kernel(
-    middle_ref,
-    skip_ref,
-    gain_ref,
-    shift_ref,
-    skipped_ref,
-    gain_out_ref,
-    shift_out_ref,
-    held_ref,
-    sems,
-):
-    copies = fetch_all(
-        [
-            (skip_ref, held_ref),
-            (gain_ref, gain_out_ref),
-            (shift_ref, shift_out_ref),
-        ],
-        sems,
-    )
-    for copy in copies:
-        copy.wait()
-    skipped_ref[...] = jnp.dot(middle_ref[...], held_ref[...], preferred_element_type=F32)
 
 
 def output_kernel(
@@ -290,12 +272,8 @@
     mid_ref,
     mixed_ref,
     done_ref,
-    held_ref,
     sems,
-    held_sem,
 ):
-    fetched = pltpu.make_async_copy(weight_ref, held_ref, held_sem)
-    fetched.start()
     total_rows, _, cols, chans = hidden_ref.shape
     rows = total_rows - 2
     scale, offset = get_affine(stats_ref, gain_ref[...], shift_ref[...], chans // GROUPS, count)
@@ -335,7 +313,7 @@
             ],
             axis=0,
         )
-        return jnp.dot(lhs, held_ref[...], preferred_element_type=F32)
+        return jnp.dot(lhs, weight_ref[...], preferred_element_type=F32)
 
     def finish(low, found):
         base = skipped_ref[low * cols : (low + 1) * cols, :]
@@ -359,8 +337,6 @@
         for row in range(filled, 2 * low + 4):
             fill(row)
         filled = 2 * low + 4
-        if low == 0:
-            fetched.wait()
         found.append(multiply(low))
     copies = []
     for low in range(rows // 2):
@@ -383,109 +359,101 @@
     dma = pltpu.SemaphoreType.DMA
     whole = jax.ShapeDtypeStruct
 
-    with jax.named_scope("stats"):
-        stats, head, tail = pl.pallas_call(
-            stats_kernel,
-            out_shape=(
-                whole((peers, 8, LANES), F32),
-                whole((1, cols, chans), BF16),
-                whole((1, cols, chans), BF16),
-            ),
-            in_specs=[far],
-            out_specs=(taken,) * 3,
-            scratch_shapes=[VMEM(latent.shape, BF16), dma((rows,))],
-            compiler_params=params(16),
-            name="stats",
-        )(in_hbm(latent))
-    with jax.named_scope("exchange_in"):
-        stats = lax.all_to_all(stats, axis, 0, 0)
-    with jax.named_scope("halo"):
-        up = lax.ppermute(tail, axis, [(i, i + 1) for i in range(ends)])
-        down = lax.ppermute(head, axis, [(i + 1, i) for i in range(ends)])
-
-    with jax.named_scope("load"):
-        ready = [gain_in.reshape(1, -1), shift_in.reshape(1, -1), conv_in]
-        ready = pl.pallas_call(
-            load_kernel,
-            out_shape=[
-                VMEM((1, chans), F32),
-                VMEM((1, chans), F32),
-                VMEM((EARLY * chans, outs), BF16),
-            ],
-            in_specs=[far] * 3,
-            out_specs=[taken] * 3,
-            scratch_shapes=[dma((3,))],
-            compiler_params=params(4),
-            cost_estimate=cost(4 << 20, 8 << 20),
-            name="load",
-        )(*map(in_hbm, ready))
-        near_gain, near_shift, near_conv = ready
-
-    with jax.named_scope("hidden"):
-        hidden, stats_mid, middle = pl.pallas_call(
-            functools.partial(
-                hidden_kernel, float(rows * cols * (chans // GROUPS) * peers), peers
-            ),
-            out_shape=(
-                whole((2 * rows + 2, 2, cols, outs), BF16),
-                whole((peers, 8, LANES), F32),
-                whole((rows * cols, chans), BF16),
-            ),
-            in_specs=[taken, taken, far, taken, taken, taken, taken, far],
-            out_specs=(taken,) * 3,
-            scratch_shapes=[
-                VMEM((rows + 2, cols, chans), BF16),
-                VMEM((9, outs // LANES, (rows + 2) * (cols + GUARD) + GUARD, LANES), F32),
-                VMEM(latent.shape, BF16),
-                VMEM(((9 - EARLY) * chans, outs), BF16),
-                dma((2,)),
-            ],
-            compiler_params=params(24),
-            name="hidden",
-        )(stats, up, in_hbm(latent), down, near_gain, near_shift, near_conv, in_hbm(conv_in))
-    with jax.named_scope("exchange_mid"):
-        stats_mid = lax.all_to_all(stats_mid, axis, 0, 0)
-
-    with jax.named_scope("skip"):
-        skipped, near_gain, near_shift = pl.pallas_call(
-            skip_kernel,
-            out_shape=[
-                VMEM((rows * cols, outs), F32),
-                VMEM((1, outs), F32),
-                VMEM((1, outs), F32),
-            ],
-            in_specs=[taken] + [far] * 3,
-            out_specs=[taken] * 3,
-            scratch_shapes=[VMEM((chans, outs), BF16), dma((3,))],
-            compiler_params=params(4),
-            cost_estimate=cost(200 << 20, 8 << 20),
-            name="skip",
-        )(
-            middle,
-            in_hbm(skip_weight),
-            in_hbm(gain_mid.reshape(1, -1)),
-            in_hbm(shift_mid.reshape(1, -1)),
-        )
-
-    with jax.named_scope("output"):
-        return pl.pallas_call(
-            functools.partial(
-                output_kernel, float(4 * rows * cols * (outs // GROUPS) * peers), peers
-            ),
-            out_shape=whole((2 * rows, 2 * cols, outs), BF16),
-            in_specs=[taken] * 4 + [far, taken],
-            out_specs=far,
-            scratch_shapes=[
-                VMEM((2 * rows + 2, cols, 4 * outs), BF16),
-                VMEM((2 * rows, outs // LANES, 2 * cols, LANES), F32),
-                VMEM((2 * rows, 2 * cols, outs), BF16),
-                VMEM(conv_mid.shape, BF16),
-                dma((2 * rows,)),
-                dma,
-            ],
-            compiler_params=params(24),
-            name="output",
-        )(stats_mid, hidden, near_gain, near_shift, in_hbm(conv_mid), skipped)
+    stats, near_row, far_row = pl.pallas_call(
+        stats_kernel,
+        out_shape=(
+            whole((peers, 8, LANES), F32),
+            whole((1, cols, chans), BF16),
+            whole((1, cols, chans), BF16),
+        ),
+        in_specs=[far],
+        out_specs=(taken,) * 3,
+        scratch_shapes=[VMEM(latent.shape, BF16), dma((rows,))],
+        compiler_params=params(16),
+        name="stats",
+    )(in_hbm(latent))
+    inner = range(1, ends)
+    far_row = lax.ppermute(far_row, axis, [(i, i + 1 if i % 2 else i - 1) for i in inner])
+    stats = lax.all_to_all(stats, axis, 0, 0)
+    near_row = lax.ppermute(near_row, axis, [(i, i ^ 1) for i in range(peers)])
+
+    ready = [latent, gain_in.reshape(1, -1), shift_in.reshape(1, -1), conv_in]
+    ready = pl.pallas_call(
+        load_kernel,
+        out_shape=[
+            VMEM(latent.shape, BF16),
+            VMEM((1, chans), F32),
+            VMEM((1, chans), F32),
+            VMEM((EARLY * chans, outs), BF16),
+        ],
+        in_specs=[far] * 4,
+        out_specs=[taken] * 4,
+        scratch_shapes=[dma((4,))],
+        compiler_params=params(4),
+        cost_estimate=cost(4 << 20, 8 << 20),
+        name="load",
+    )(*map(in_hbm, ready))
+    near_latent, near_gain, near_shift, near_conv = ready
+
+    hidden, stats_mid, skipped = pl.pallas_call(
+        functools.partial(
+            hidden_kernel, float(rows * cols * (chans // GROUPS) * peers), peers
+        ),
+        out_shape=(
+            whole((2 * rows + 2, 2, cols, outs), BF16),
+            whole((peers, 8, LANES), F32),
+            whole((rows * cols, outs), F32),
+        ),
+        in_specs=[taken] * 7 + [far] * 2,
+        out_specs=(taken,) * 3,
+        scratch_shapes=[
+            VMEM((rows + 2, cols, chans), BF16),
+            VMEM((9, outs // LANES, (rows + 2) * (cols + GUARD) + GUARD, LANES), F32),
+            VMEM(((9 - EARLY) * chans, outs), BF16),
+            VMEM((chans, outs), BF16),
+            dma((2,)),
+        ],
+        compiler_params=params(24),
+        name="hidden",
+    )(
+        stats,
+        near_row,
+        far_row,
+        near_latent,
+        near_gain,
+        near_shift,
+        near_conv,
+        in_hbm(conv_in),
+        in_hbm(skip_weight),
+    )
+    stats_mid = lax.all_to_all(stats_mid, axis, 0, 0)
+
+    ready = [gain_mid.reshape(1, -1), shift_mid.reshape(1, -1), conv_mid]
+    near_gain, near_shift, near_mid = pl.pallas_call(
+        load_kernel,
+        out_shape=[VMEM(part.shape, part.dtype) for part in ready],
+        in_specs=[far] * 3,
+        out_specs=[taken] * 3,
+        scratch_shapes=[dma((3,))],
+        compiler_params=params(4),
+        cost_estimate=cost(4 << 20, 8 << 20),
+        name="load_mid",
+    )(*map(in_hbm, ready))
+
+    return pl.pallas_call(
+        functools.partial(output_kernel, float(4 * rows * cols * (outs // GROUPS) * peers), peers),
+        out_shape=whole((2 * rows, 2 * cols, outs), BF16),
+        in_specs=[taken] * 6,
+        out_specs=far,
+        scratch_shapes=[
+            VMEM((2 * rows + 2, cols, 4 * outs), BF16),
+            VMEM((2 * rows, outs // LANES, 2 * cols, LANES), F32),
+            VMEM((2 * rows, 2 * cols, outs), BF16),
+            dma((2 * rows,)),
+        ],
+        compiler_params=params(24),
+        name="output",
+    )(stats_mid, hidden, near_gain, near_shift, near_mid, skipped)
 
 
 def solution(mesh):

time: 42.9 us -> 38.7 us (0.902)
  starting transfers between devices: 16.5 us -> 13.5 us
  Pallas kernels: 14.7 us -> 13.5 us
    ppermute x2, starting transfers between devices: 3.7 us -> 1.22 us  [the longest x1 0.67 us: body(): lax.ppermute(far_row, axis, [(i, i + 1 if i % 2 else i - 1) for i in inner])]
    pallas_call x1, Pallas kernels: 5.21 us -> 4.15 us  [body(): pl.pallas_call(functools.partial(output_kernel, float(4 * rows * cols * (...]
    all_to_all x1, starting transfers between devices: 9.26 us -> 8.79 us  [body(): stats = lax.all_to_all(stats, axis, 0, 0)]
  transfers between devices with their start and end apart: 4 -> 4, of which waited for: 2 -> 2; matrix products, arithmetic and copies ran while one was open for 0% -> 0% of each run, Pallas kernels for 6% -> 7%
where the time goes in v5:
time: 38.7 us; the launch traced here: 38.4 us
  Pallas kernels  13.5 us (35%)
  starting transfers between devices  13.5 us (35%)
  waiting for transfers between devices  11.2 us (29%)
    all_to_all x1, starting transfers between devices, body(): stats = lax.all_to_all(stats, axis, 0, 0)  8.79 us
    all_to_all x1, waiting for transfers between devices, body(): stats = lax.all_to_all(stats, axis, 0, 0)  5.71 us
    all_to_all x1, waiting for transfers between devices, body(): stats_mid = lax.all_to_all(stats_mid, axis, 0, 0)  5.52 us
    pallas_call x1, Pallas kernels, body(): pl.pallas_call(functools.partial(hidden_kernel, float(rows * cols * (chan...  5.13 us
    pallas_call x1, Pallas kernels, body(): pl.pallas_call(functools.partial(output_kernel, float(4 * rows * cols * (...  4.15 us
    all_to_all x1, starting transfers between devices, body(): stats_mid = lax.all_to_all(stats_mid, axis, 0, 0)  3.51 us
    pallas_call x1, Pallas kernels, body(): pl.pallas_call(stats_kernel, out_shape=(whole((peers, 8, LANES), F32), wh...  1.75 us
    pallas_call x1, Pallas kernels, body(): pl.pallas_call(load_kernel, out_shape=[VMEM(part.shape, part.dtype) for p...  1.33 us
  transfers between devices with their start and end apart: 4, of which 2 were waited for; matrix products, arithmetic and copies ran while one was open for 0% of the time, Pallas kernels for 7%

profile of v5, /device:TPU:0, one launch (start us, length us, event | category | flops | bytes accessed | tf_op | source)
XLA Modules:
  0.0 38.4 jit_solution(932577895018270777)
XLA Ops:
  0.0 1.7 %stats.1 = (f32[16,8,128]{2,1,0:T(8,128)}, bf16[1,256,512]{2,1,0:T(8,128)(2,1)S(1)}, bf16[1,256,512]{2,1,0:T(8,128)(2,1)S(1)}) custom-call(bf16[2,256,512]{2,1,0:T(8,128)(2,1)} %refs_0_.1), custom_call_target="tpu_custom_call" | custom-call | tf_op jit(solution)/shard_map/stats/pallas_call | solution.py:362
  1.8 0.6 %collective-permute-start = (bf16[1,256,512]{2,1,0:T(8,128)(2,1)S(1)}, bf16[1,256,512]{2,1,0:T(8,128)(2,1)S(1)}, u32[]{:S(2)}, u32[]{:S(2)}) collective-permute-start(bf16[1,256,512]{2,1,0:T(8,128)(2,1)S(1)} %get-tuple-element.19), channel_id=1, source_target_pairs={{0,1},{1,0},{2,3},{3,2},{4,5},{5,4},{6,7},{7,6},{8,9},{9,8},{10,11... | collective-permute-start | bytes 786440 | tf_op jit(solution)/shard_map/ppermute | solution.py:378
  2.3 0.7 %collective-permute-start.1 = (bf16[1,256,512]{2,1,0:T(8,128)(2,1)S(1)}, bf16[1,256,512]{2,1,0:T(8,128)(2,1)S(1)}, u32[]{:S(2)}, u32[]{:S(2)}) collective-permute-start(bf16[1,256,512]{2,1,0:T(8,128)(2,1)S(1)} %get-tuple-element.20), channel_id=1, source_target_pairs={{1,2},{2,1},{3,4},{4,3},{5,6},{6,5},{7,8},{8,7},{9,10},{10,9},{11,... | collective-permute-start | bytes 786440 | tf_op jit(solution)/shard_map/ppermute | solution.py:376
  3.0 8.8 %all-to-all-start = ((f32[16,8,128]{2,1,0:T(8,128)}), f32[16,8,128]{2,1,0:T(8,128)S(1)}, u32[]{:S(2)}, u32[]{:S(2)}) async-start(f32[16,8,128]{2,1,0:T(8,128)} %get-tuple-element.18), calls=%async_computation | async-start | bytes 131072 | tf_op jit(solution)/shard_map/all_to_all | solution.py:377
  11.8 1.2 %load.1 = (bf16[2,256,512]{2,1,0:T(8,128)(2,1)S(1)}, f32[1,512]{1,0:T(1,128)S(1)}, f32[1,512]{1,0:T(1,128)S(1)}, bf16[512,256]{1,0:T(8,128)(2,1)S(1)}) custom-call(bf16[2,256,512]{2,1,0:T(8,128)(2,1)} %refs_0_.1, f32[1,512]{1,0:T(1,128)} %bitcast.4, f32[1,512]{1,0:T(1,128)} %bitcast.5, bf16[4608,256]{1,0:T(8,128)(2,1)} %rest_ref.1), custom_call_target="tpu_custom_call" | custom-call | flops 4194304 | bytes 8388608 | tf_op jit(solution)/shard_map/load/pallas_call | solution.py:381
  13.0 5.7 %all-to-all-done.stats_ref = f32[16,8,128]{2,1,0:T(8,128)S(1)} async-done(((f32[16,8,128]{2,1,0:T(8,128)}), f32[16,8,128]{2,1,0:T(8,128)S(1)}, u32[]{:S(2)}, u32[]{:S(2)}) %all-to-all-start) | async-done | bytes 65568 | tf_op jit(solution)/shard_map/all_to_all | solution.py:377
  18.7 0.0 collective-permute-done.near_row_ref
  18.7 0.0 collective-permute-done.1.far_row_ref
  18.7 5.1 %hidden.1 = (bf16[6,2,256,256]{3,2,1,0:T(8,128)(2,1)S(1)}, f32[16,8,128]{2,1,0:T(8,128)}, f32[512,256]{1,0:T(8,128)S(1)}) custom-call(f32[16,8,128]{2,1,0:T(8,128)S(1)} %all-to-all-done.stats_ref, bf16[1,256,512]{2,1,0:T(8,128)(2,1)S(1)} %collective-permute-done.near_row_ref, bf16[1,256,512]{2,1,0:T(8,128)(2,1)S(1)} %collective-permute-done.1.far_row_ref, ...), custom_call_target="tpu_custom_call" | custom-call | tf_op jit(solution)/shard_map/hidden/pallas_call | solution.py:398
  23.8 3.5 %all-to-all-start.1 = ((f32[16,8,128]{2,1,0:T(8,128)}), f32[16,8,128]{2,1,0:T(8,128)S(1)}, u32[]{:S(2)}, u32[]{:S(2)}) async-start(f32[16,8,128]{2,1,0:T(8,128)} %get-tuple-element.25), calls=%async_computation.1 | async-start | bytes 131072 | tf_op jit(solution)/shard_map/all_to_all | solution.py:429
  27.3 1.3 %load_mid.1 = (f32[1,256]{1,0:T(1,128)S(1)}, f32[1,256]{1,0:T(1,128)S(1)}, bf16[2304,256]{1,0:T(8,128)(2,1)S(1)}) custom-call(f32[1,256]{1,0:T(1,128)} %bitcast.6, f32[1,256]{1,0:T(1,128)} %bitcast.7, bf16[2304,256]{1,0:T(8,128)(2,1)} %refs_2_.1), custom_call_target="tpu_custom_call" | custom-call | flops 4194304 | bytes 8388608 | tf_op jit(solution)/shard_map/load_mid/pallas_call | solution.py:432
  28.7 5.5 %all-to-all-done.1.stats_ref = f32[16,8,128]{2,1,0:T(8,128)S(1)} async-done(((f32[16,8,128]{2,1,0:T(8,128)}), f32[16,8,128]{2,1,0:T(8,128)S(1)}, u32[]{:S(2)}, u32[]{:S(2)}) %all-to-all-start.1) | async-done | bytes 65568 | tf_op jit(solution)/shard_map/all_to_all | solution.py:429
  34.2 4.2 %output.1 = bf16[4,512,256]{2,1,0:T(8,128)(2,1)} custom-call(f32[16,8,128]{2,1,0:T(8,128)S(1)} %all-to-all-done.1.stats_ref, bf16[6,2,256,256]{3,2,1,0:T(8,128)(2,1)S(1)} %get-tuple-element.26.hidden_ref, f32[1,256]{1,0:T(1,128)S(1)} %get-tuple-element.27.gain_ref, f32[1,256]{1,0:T(1,128)S(1)} %get-tuple-element.28.shift_ref, ...), custom_call_target="tpu_custom_call" | custom-call | tf_op jit(solution)/shard_map/output/pallas_call | solution.py:443
Async XLA Ops:
  1.8 16.9 %collective-permute-start = (bf16[1,256,512]{2,1,0:T(8,128)(2,1)S(1)}, bf16[1,256,512]{2,1,0:T(8,128)(2,1)S(1)}, u32[]{:S(2)}, u32[]{:S(2)}) collective-permute-start(bf16[1,256,512]{2,1,0:T(8,128)(2,1)S(1)} %get-tuple-element.19), channel_id=1, source_target_pairs={{0,1},{1,0},{2,3},{3,2},{4,5},{5,4},{6,7},{7,6},{8,9},{9,8},{10,11... | collective-permute-start | bytes 786440 | tf_op jit(solution)/shard_map/ppermute | solution.py:378
  2.3 16.4 %collective-permute-start.1 = (bf16[1,256,512]{2,1,0:T(8,128)(2,1)S(1)}, bf16[1,256,512]{2,1,0:T(8,128)(2,1)S(1)}, u32[]{:S(2)}, u32[]{:S(2)}) collective-permute-start(bf16[1,256,512]{2,1,0:T(8,128)(2,1)S(1)} %get-tuple-element.20), channel_id=1, source_target_pairs={{1,2},{2,1},{3,4},{4,3},{5,6},{6,5},{7,8},{8,7},{9,10},{10,9},{11,... | collective-permute-start | bytes 786440 | tf_op jit(solution)/shard_map/ppermute | solution.py:376
  3.0 15.7 %all-to-all-start = ((f32[16,8,128]{2,1,0:T(8,128)}), f32[16,8,128]{2,1,0:T(8,128)S(1)}, u32[]{:S(2)}, u32[]{:S(2)}) async-start(f32[16,8,128]{2,1,0:T(8,128)} %get-tuple-element.18), calls=%async_computation | async-start | bytes 131072 | tf_op jit(solution)/shard_map/all_to_all | solution.py:377
  23.8 10.4 %all-to-all-start.1 = ((f32[16,8,128]{2,1,0:T(8,128)}), f32[16,8,128]{2,1,0:T(8,128)S(1)}, u32[]{:S(2)}, u32[]{:S(2)}) async-start(f32[16,8,128]{2,1,0:T(8,128)} %get-tuple-element.25), calls=%async_computation.1 | async-start | bytes 131072 | tf_op jit(solution)/shard_map/all_to_all | solution.py:429

commit v6 on v5

--- a/solution.py
+++ b/solution.py
@@ -15,7 +15,6 @@
 LANES = 128
 GUARD = 8
 SPLIT = 2
-EARLY = 1
 STEP = 16
 VMEM = pltpu.VMEM
 
@@ -129,28 +128,20 @@
     gain_ref,
     shift_ref,
     weight_ref,
-    rest_ref,
-    skip_ref,
     hidden_ref,
     out_ref,
-    skipped_ref,
+    affine_ref,
     act_ref,
     tap_ref,
-    late_ref,
-    skips_ref,
-    sems,
 ):
     rows, cols, chans = latent_ref.shape
     outs = weight_ref.shape[1]
-    split = EARLY * chans
-    fetched = fetch_all(
-        [(rest_ref.at[pl.ds(split, (9 - EARLY) * chans), :], late_ref), (skip_ref, skips_ref)],
-        sems,
-    )
     halves = outs // LANES
     pitch = cols + GUARD
     part = cols // SPLIT
     scale, offset = get_affine(stats_ref, gain_ref[...], shift_ref[...], chans // GROUPS, count)
+    affine_ref[0] = scale
+    affine_ref[1] = offset
     place = lax.axis_index("rows")
     odd = lax.rem(place, 2) == 1
     total_rows = 2 * rows + 2
@@ -182,10 +173,7 @@
     def multiply(piece, taps):
         span = slice(piece * part, (piece + 1) * part)
         for tap in taps:
-            if tap < EARLY:
-                weight = weight_ref[tap * chans : (tap + 1) * chans, :]
-            else:
-                weight = late_ref[(tap - EARLY) * chans : (tap + 1 - EARLY) * chans, :]
+            weight = weight_ref[tap * chans : (tap + 1) * chans, :]
             used = [source[tap // 3] for source in sources]
             first, last = min(used), max(used) + 1
             found = jnp.dot(
@@ -239,14 +227,7 @@
     ready[-1] = chunks
     for piece in range(SPLIT):
         fill(piece, range(rows + 2))
-        multiply(piece, range(EARLY))
-    for copy in fetched:
-        copy.wait()
-    for piece in range(SPLIT):
-        multiply(piece, range(EARLY, 9))
-    skipped_ref[...] = jnp.dot(
-        act_ref[1 : rows + 1].reshape(-1, chans), skips_ref[...], preferred_element_type=F32
-    )
+        multiply(piece, range(9))
     done = 0
     for piece in range(SPLIT):
         for chunk in range(done, ready[piece]):
@@ -257,6 +238,40 @@
         jnp.concatenate([jnp.sum(t, axis=0, keepdims=True) for t in totals], axis=1),
         jnp.concatenate([jnp.sum(t, axis=0, keepdims=True) for t in squares], axis=1),
     )
+
+
+def skip_kernel(
+    affine_ref,
+    gain_ref,
+    shift_ref,
+    weight_ref,
+    latent_ref,
+    skip_ref,
+    gain_out_ref,
+    shift_out_ref,
+    weight_out_ref,
+    skipped_ref,
+    near_ref,
+    held_ref,
+    sems,
+):
+    copies = fetch_all(
+        [
+            (latent_ref, near_ref),
+            (skip_ref, held_ref),
+            (gain_ref, gain_out_ref),
+            (shift_ref, shift_out_ref),
+            (weight_ref, weight_out_ref),
+        ],
+        sems,
+    )
+    copies[0].wait()
+    copies[1].wait()
+    values = near_ref[...].astype(F32).reshape(-1, near_ref.shape[2])
+    act = half_silu(values, affine_ref[0], affine_ref[1]).astype(BF16)
+    skipped_ref[...] = jnp.dot(act, held_ref[...], preferred_element_type=F32)
+    for copy in copies[2:]:
+        copy.wait()
 
 
 def output_kernel(
@@ -315,6 +330,8 @@
         )
         return jnp.dot(lhs, weight_ref[...], preferred_element_type=F32)
 
+    copies = []
+
     def finish(low, found):
         base = skipped_ref[low * cols : (low + 1) * cols, :]
         for side in range(2):
@@ -330,6 +347,8 @@
                 done_ref[row, :, half * LANES : (half + 1) * LANES] = mixed_ref[row, half].astype(
                     BF16
                 )
+            copies.append(pltpu.make_async_copy(done_ref.at[row], out_ref.at[row], sems.at[row]))
+            copies[-1].start()
 
     found = []
     filled = 0
@@ -338,14 +357,26 @@
             fill(row)
         filled = 2 * low + 4
         found.append(multiply(low))
-    copies = []
     for low in range(rows // 2):
         finish(low, found[low])
-        for row in (2 * low, 2 * low + 1):
-            copies.append(pltpu.make_async_copy(done_ref.at[row], out_ref.at[row], sems.at[row]))
-            copies[-1].start()
     for copy in copies:
         copy.wait()
+
+
+def exchange(values, axis):
+    peers = lax.axis_size(axis)
+    if peers & (peers - 1):
+        return lax.psum(values, axis)
+    step = 1
+    while step < peers:
+        radix = 2 if peers // step == 2 else 4
+        parts = [
+            lax.ppermute(values, axis, [(i, i ^ (step * k)) for i in range(peers)])
+            for k in range(1, radix)
+        ]
+        values = sum(parts, values)
+        step *= radix
+    return values
 
 
 def body(latent, gain_in, shift_in, conv_in, gain_mid, shift_mid, conv_mid, skip_weight):
@@ -384,7 +415,7 @@
             VMEM(latent.shape, BF16),
             VMEM((1, chans), F32),
             VMEM((1, chans), F32),
-            VMEM((EARLY * chans, outs), BF16),
+            VMEM(conv_in.shape, BF16),
         ],
         in_specs=[far] * 4,
         out_specs=[taken] * 4,
@@ -395,23 +426,20 @@
     )(*map(in_hbm, ready))
     near_latent, near_gain, near_shift, near_conv = ready
 
-    hidden, stats_mid, skipped = pl.pallas_call(
+    hidden, stats_mid, affine = pl.pallas_call(
         functools.partial(
             hidden_kernel, float(rows * cols * (chans // GROUPS) * peers), peers
         ),
         out_shape=(
             whole((2 * rows + 2, 2, cols, outs), BF16),
-            whole((peers, 8, LANES), F32),
-            whole((rows * cols, outs), F32),
+            whole((1, 8, LANES), F32),
+            VMEM((2, 1, chans), F32),
         ),
-        in_specs=[taken] * 7 + [far] * 2,
+        in_specs=[taken] * 7,
         out_specs=(taken,) * 3,
         scratch_shapes=[
             VMEM((rows + 2, cols, chans), BF16),
             VMEM((9, outs // LANES, (rows + 2) * (cols + GUARD) + GUARD, LANES), F32),
-            VMEM(((9 - EARLY) * chans, outs), BF16),
-            VMEM((chans, outs), BF16),
-            dma((2,)),
         ],
         compiler_params=params(24),
         name="hidden",
@@ -423,22 +451,31 @@
         near_gain,
         near_shift,
         near_conv,
-        in_hbm(conv_in),
+    )
+    stats_mid = exchange(stats_mid, axis)
+
+    near_gain, near_shift, near_mid, skipped = pl.pallas_call(
+        skip_kernel,
+        out_shape=(
+            VMEM((1, outs), F32),
+            VMEM((1, outs), F32),
+            VMEM(conv_mid.shape, BF16),
+            whole((rows * cols, outs), F32),
+        ),
+        in_specs=[taken] + [far] * 5,
+        out_specs=(taken,) * 4,
+        scratch_shapes=[VMEM(latent.shape, BF16), VMEM((chans, outs), BF16), dma((5,))],
+        compiler_params=params(16),
+        cost_estimate=cost(200 << 20, 8 << 20),
+        name="skip",
+    )(
+        affine,
+        in_hbm(gain_mid.reshape(1, -1)),
+        in_hbm(shift_mid.reshape(1, -1)),
+        in_hbm(conv_mid),
+        in_hbm(latent),
         in_hbm(skip_weight),
     )
-    stats_mid = lax.all_to_all(stats_mid, axis, 0, 0)
-
-    ready = [gain_mid.reshape(1, -1), shift_mid.reshape(1, -1), conv_mid]
-    near_gain, near_shift, near_mid = pl.pallas_call(
-        load_kernel,
-        out_shape=[VMEM(part.shape, part.dtype) for part in ready],
-        in_specs=[far] * 3,
-        out_specs=[taken] * 3,
-        scratch_shapes=[dma((3,))],
-        compiler_params=params(4),
-        cost_estimate=cost(4 << 20, 8 << 20),
-        name="load_mid",
-    )(*map(in_hbm, ready))
 
     return pl.pallas_call(
         functools.partial(output_kernel, float(4 * rows * cols * (outs // GROUPS) * peers), peers),

time: 38.7 us -> 36.2 us (0.935)
  waiting for transfers between devices: 11.2 us -> 6.81 us
  starting transfers between devices: 13.5 us -> 16.4 us
  Pallas kernels: 13.5 us -> 12.6 us
    ppermute x0 -> x6, starting transfers between devices: none -> 6.37 us  [exchange(): lax.ppermute(values, axis, [(i, i ^ step * k) for i in range(peers)])]
    all_to_all x1 -> x0, waiting for transfers between devices: 5.52 us -> none  [body(): stats_mid = lax.all_to_all(stats_mid, axis, 0, 0)]
    all_to_all x1 -> x0, starting transfers between devices: 3.51 us -> none  [body(): stats_mid = lax.all_to_all(stats_mid, axis, 0, 0)]
    pallas_call x1, Pallas kernels: 5.13 us -> 3.14 us  [body(): pl.pallas_call(functools.partial(hidden_kernel, float(rows * cols * (chan...]
    ppermute x0 -> x6, waiting for transfers between devices: none -> 1.83 us  [exchange(): lax.ppermute(values, axis, [(i, i ^ step * k) for i in range(peers)])]
    all_to_all x1, waiting for transfers between devices: 5.71 us -> 4.98 us  [body(): stats = lax.all_to_all(stats, axis, 0, 0)]
    pallas_call x1, Pallas kernels: 1.18 us -> 1.91 us  [body(): pl.pallas_call(load_kernel, out_shape=[VMEM(latent.shape, BF16), VMEM((1,...]
  transfers between devices with their start and end apart: 4 -> 9, of which waited for: 2 -> 3; matrix products, arithmetic and copies ran while one was open for 0% -> 0% of each run, Pallas kernels for 7% -> 10%
where the time goes in v6:
time: 36.2 us; the launch traced here: 35.9 us
  starting transfers between devices  16.4 us (45%)
  Pallas kernels  12.6 us (35%)
  waiting for transfers between devices  6.81 us (19%)
    all_to_all x1, starting transfers between devices, body(): stats = lax.all_to_all(stats, axis, 0, 0)  8.78 us
    ppermute x6, starting transfers between devices, exchange(): lax.ppermute(values, axis, [(i, i ^ step * k) for i in range(peers)])  6.37 us
    all_to_all x1, waiting for transfers between devices, body(): stats = lax.all_to_all(stats, axis, 0, 0)  4.98 us
    pallas_call x1, Pallas kernels, body(): pl.pallas_call(functools.partial(output_kernel, float(4 * rows * cols * (...  4.1 us
    pallas_call x1, Pallas kernels, body(): pl.pallas_call(functools.partial(hidden_kernel, float(rows * cols * (chan...  3.14 us
    pallas_call x1, Pallas kernels, body(): pl.pallas_call(load_kernel, out_shape=[VMEM(latent.shape, BF16), VMEM((1,...  1.91 us
    pallas_call x1, Pallas kernels, body(): pl.pallas_call(stats_kernel, out_shape=(whole((peers, 8, LANES), F32), wh...  1.86 us
    ppermute x6, waiting for transfers between devices, exchange(): lax.ppermute(values, axis, [(i, i ^ step * k) for i in range(peers)])  1.83 us
  transfers between devices with their start and end apart: 9, of which 3 were waited for; matrix products, arithmetic and copies ran while one was open for 0% of the time, Pallas kernels for 10%

profile of v6, /device:TPU:0, one launch (start us, length us, event | category | flops | bytes accessed | tf_op | source)
XLA Modules:
  0.0 35.9 jit_solution(2721457183669985060)
XLA Ops:
  0.0 1.9 %stats.1 = (f32[16,8,128]{2,1,0:T(8,128)}, bf16[1,256,512]{2,1,0:T(8,128)(2,1)}, bf16[1,256,512]{2,1,0:T(8,128)(2,1)}) custom-call(bf16[2,256,512]{2,1,0:T(8,128)(2,1)} %latent_ref.3), custom_call_target="tpu_custom_call" | custom-call | tf_op jit(solution)/shard_map/stats/pallas_call | solution.py:393
  1.9 0.6 %collective-permute-start = (bf16[1,256,512]{2,1,0:T(8,128)(2,1)}, bf16[1,256,512]{2,1,0:T(8,128)(2,1)S(1)}, u32[]{:S(2)}, u32[]{:S(2)}) collective-permute-start(bf16[1,256,512]{2,1,0:T(8,128)(2,1)} %get-tuple-element.20), channel_id=1, source_target_pairs={{0,1},{1,0},{2,3},{3,2},{4,5},{5,4},{6,7},{7,6},{8,9},{9,8},{10,11... | collective-permute-start | bytes 786440 | tf_op jit(solution)/shard_map/ppermute | solution.py:409
  2.4 0.7 %collective-permute-start.1 = (bf16[1,256,512]{2,1,0:T(8,128)(2,1)}, bf16[1,256,512]{2,1,0:T(8,128)(2,1)S(1)}, u32[]{:S(2)}, u32[]{:S(2)}) collective-permute-start(bf16[1,256,512]{2,1,0:T(8,128)(2,1)} %get-tuple-element.21), channel_id=1, source_target_pairs={{1,2},{2,1},{3,4},{4,3},{5,6},{6,5},{7,8},{8,7},{9,10},{10,9},{11,... | collective-permute-start | bytes 786440 | tf_op jit(solution)/shard_map/ppermute | solution.py:407
  3.1 8.8 %all-to-all-start = ((f32[16,8,128]{2,1,0:T(8,128)}), f32[16,8,128]{2,1,0:T(8,128)S(1)}, u32[]{:S(2)}, u32[]{:S(2)}) async-start(f32[16,8,128]{2,1,0:T(8,128)} %get-tuple-element.19), calls=%async_computation | async-start | bytes 131072 | tf_op jit(solution)/shard_map/all_to_all | solution.py:408
  11.9 1.9 %load.1 = (bf16[2,256,512]{2,1,0:T(8,128)(2,1)S(1)}, f32[1,512]{1,0:T(1,128)S(1)}, f32[1,512]{1,0:T(1,128)S(1)}, bf16[4608,256]{1,0:T(8,128)(2,1)S(1)}) custom-call(bf16[2,256,512]{2,1,0:T(8,128)(2,1)} %latent_ref.3, f32[1,512]{1,0:T(1,128)} %bitcast.4, f32[1,512]{1,0:T(1,128)} %bitcast.5, bf16[4608,256]{1,0:T(8,128)(2,1)} %refs_3_.1), custom_call_target="tpu_custom_call" | custom-call | flops 4194304 | bytes 8388608 | tf_op jit(solution)/shard_map/load/pallas_call | solution.py:412
  13.8 5.0 %all-to-all-done.stats_ref = f32[16,8,128]{2,1,0:T(8,128)S(1)} async-done(((f32[16,8,128]{2,1,0:T(8,128)}), f32[16,8,128]{2,1,0:T(8,128)S(1)}, u32[]{:S(2)}, u32[]{:S(2)}) %all-to-all-start) | async-done | bytes 65568 | tf_op jit(solution)/shard_map/all_to_all | solution.py:408
  18.8 0.0 collective-permute-done.near_row_ref
  18.8 0.0 collective-permute-done.1.far_row_ref
  18.8 3.1 %hidden.1 = (bf16[6,2,256,256]{3,2,1,0:T(8,128)(2,1)S(1)}, f32[1,8,128]{2,1,0:T(8,128)S(1)}, f32[2,1,512]{2,1,0:T(1,128)S(1)}) custom-call(f32[16,8,128]{2,1,0:T(8,128)S(1)} %all-to-all-done.stats_ref, bf16[1,256,512]{2,1,0:T(8,128)(2,1)S(1)} %collective-permute-done.near_row_ref, bf16[1,256,512]{2,1,0:T(8,128)(2,1)S(1)} %collective-permute-done.1.far_row_ref, ...), custom_call_target="tpu_custom_call" | custom-call | tf_op jit(solution)/shard_map/hidden/pallas_call | solution.py:429
  21.9 0.1 collective-permute-start.4
  22.0 1.2 %collective-permute-start.3 = (f32[1,8,128]{2,1,0:T(8,128)S(1)}, f32[1,8,128]{2,1,0:T(8,128)S(1)}, u32[]{:S(2)}, u32[]{:S(2)}) collective-permute-start(f32[1,8,128]{2,1,0:T(8,128)S(1)} %get-tuple-element.26), channel_id=1, source_target_pairs={{0,2},{1,3},{2,0},{3,1},{4,6},{5,7},{6,4},{7,5},{8,10},{9,11},{10,... | collective-permute-start | bytes 12296 | tf_op jit(solution)/shard_map/ppermute | solution.py:374
  23.2 0.7 %collective-permute-start.2 = (f32[1,8,128]{2,1,0:T(8,128)S(1)}, f32[1,8,128]{2,1,0:T(8,128)S(1)}, u32[]{:S(2)}, u32[]{:S(2)}) collective-permute-start(f32[1,8,128]{2,1,0:T(8,128)S(1)} %get-tuple-element.26), channel_id=1, source_target_pairs={{0,1},{1,0},{2,3},{3,2},{4,5},{5,4},{6,7},{7,6},{8,9},{9,8},{10,11... | collective-permute-start | bytes 12296 | tf_op jit(solution)/shard_map/ppermute | solution.py:374
  23.9 1.2 %collective-permute-done.4 = f32[1,8,128]{2,1,0:T(8,128)S(1)} collective-permute-done((f32[1,8,128]{2,1,0:T(8,128)S(1)}, f32[1,8,128]{2,1,0:T(8,128)S(1)}, u32[]{:S(2)}, u32[]{:S(2)}) %collective-permute-start.4) | collective-permute-done | bytes 4128 | tf_op jit(solution)/shard_map/ppermute | solution.py:374
  25.0 0.7 %collective-permute-done.3 = f32[1,8,128]{2,1,0:T(8,128)S(1)} collective-permute-done((f32[1,8,128]{2,1,0:T(8,128)S(1)}, f32[1,8,128]{2,1,0:T(8,128)S(1)}, u32[]{:S(2)}, u32[]{:S(2)}) %collective-permute-start.3) | collective-permute-done | bytes 4128 | tf_op jit(solution)/shard_map/ppermute | solution.py:374
  25.7 0.0 collective-permute-done.2
  25.7 0.9 %collective-permute-start.7 = (f32[1,8,128]{2,1,0:T(8,128)S(1)}, f32[1,8,128]{2,1,0:T(8,128)S(1)}, u32[]{:S(2)}, u32[]{:S(2)}) collective-permute-start(f32[1,8,128]{2,1,0:T(8,128)S(1)} %add_add_fusion.1), channel_id=1, source_target_pairs={{0,12},{1,13},{2,14},{3,15},{4,8},{5,9},{6,10},{7,11},{8,4},{9,5},... | collective-permute-start | bytes 12296 | tf_op jit(solution)/shard_map/ppermute | solution.py:374
  26.6 1.0 %collective-permute-start.6 = (f32[1,8,128]{2,1,0:T(8,128)S(1)}, f32[1,8,128]{2,1,0:T(8,128)S(1)}, u32[]{:S(2)}, u32[]{:S(2)}) collective-permute-start(f32[1,8,128]{2,1,0:T(8,128)S(1)} %add_add_fusion.1), channel_id=1, source_target_pairs={{0,8},{1,9},{2,10},{3,11},{4,12},{5,13},{6,14},{7,15},{8,0},{9,1},... | collective-permute-start | bytes 12296 | tf_op jit(solution)/shard_map/ppermute | solution.py:374
  27.6 2.5 %collective-permute-start.5 = (f32[1,8,128]{2,1,0:T(8,128)S(1)}, f32[1,8,128]{2,1,0:T(8,128)S(1)}, u32[]{:S(2)}, u32[]{:S(2)}) collective-permute-start(f32[1,8,128]{2,1,0:T(8,128)S(1)} %add_add_fusion.1), channel_id=1, source_target_pairs={{0,4},{1,5},{2,6},{3,7},{4,0},{5,1},{6,2},{7,3},{8,12},{9,13},{10,... | collective-permute-start | bytes 12296 | tf_op jit(solution)/shard_map/ppermute | solution.py:374
  30.2 1.6 %skip.1 = (f32[1,256]{1,0:T(1,128)S(1)}, f32[1,256]{1,0:T(1,128)S(1)}, bf16[2304,256]{1,0:T(8,128)(2,1)S(1)}, f32[512,256]{1,0:T(8,128)S(1)}) custom-call(f32[2,1,512]{2,1,0:T(1,128)S(1)} %get-tuple-element.28.affine_ref, f32[1,256]{1,0:T(1,128)} %bitcast.6, f32[1,256]{1,0:T(1,128)} %bitcast.7, bf16[2304,256]{1,0:T(8,128)(2,1)} %weight_ref.1, ...), custom_call_target="tpu_custom_call" | custom-call | flops 209715200 | bytes 8388608 | tf_op jit(solution)/shard_map/skip/pallas_call | solution.py:457
  31.8 0.0 collective-permute-done.7
  31.8 0.0 collective-permute-done.6
  31.8 0.0 collective-permute-done.5
  31.8 4.1 %output.1 = bf16[4,512,256]{2,1,0:T(8,128)(2,1)} custom-call(f32[1,8,128]{2,1,0:T(8,128)S(1)} %add_add_fusion.stats_ref, bf16[6,2,256,256]{3,2,1,0:T(8,128)(2,1)S(1)} %get-tuple-element.27.hidden_ref, f32[1,256]{1,0:T(1,128)S(1)} %get-tuple-element.29.gain_ref, f32[1,256]{1,0:T(1,128)S(1)} %get-tuple-element.30.shift_ref, ...), custom_call_target="tpu_custom_call" | custom-call | tf_op jit(solution)/shard_map/output/pallas_call | solution.py:480
  (2 shorter events, 0.0 us)
Async XLA Ops:
  1.9 16.9 %collective-permute-start = (bf16[1,256,512]{2,1,0:T(8,128)(2,1)}, bf16[1,256,512]{2,1,0:T(8,128)(2,1)S(1)}, u32[]{:S(2)}, u32[]{:S(2)}) collective-permute-start(bf16[1,256,512]{2,1,0:T(8,128)(2,1)} %get-tuple-element.20), channel_id=1, source_target_pairs={{0,1},{1,0},{2,3},{3,2},{4,5},{5,4},{6,7},{7,6},{8,9},{9,8},{10,11... | collective-permute-start | bytes 786440 | tf_op jit(solution)/shard_map/ppermute | solution.py:409
  2.4 16.4 %collective-permute-start.1 = (bf16[1,256,512]{2,1,0:T(8,128)(2,1)}, bf16[1,256,512]{2,1,0:T(8,128)(2,1)S(1)}, u32[]{:S(2)}, u32[]{:S(2)}) collective-permute-start(bf16[1,256,512]{2,1,0:T(8,128)(2,1)} %get-tuple-element.21), channel_id=1, source_target_pairs={{1,2},{2,1},{3,4},{4,3},{5,6},{6,5},{7,8},{8,7},{9,10},{10,9},{11,... | collective-permute-start | bytes 786440 | tf_op jit(solution)/shard_map/ppermute | solution.py:407
  3.1 15.7 %all-to-all-start = ((f32[16,8,128]{2,1,0:T(8,128)}), f32[16,8,128]{2,1,0:T(8,128)S(1)}, u32[]{:S(2)}, u32[]{:S(2)}) async-start(f32[16,8,128]{2,1,0:T(8,128)} %get-tuple-element.19), calls=%async_computation | async-start | bytes 131072 | tf_op jit(solution)/shard_map/all_to_all | solution.py:408
  21.9 3.1 %collective-permute-start.4 = (f32[1,8,128]{2,1,0:T(8,128)S(1)}, f32[1,8,128]{2,1,0:T(8,128)S(1)}, u32[]{:S(2)}, u32[]{:S(2)}) collective-permute-start(f32[1,8,128]{2,1,0:T(8,128)S(1)} %get-tuple-element.26), channel_id=1, source_target_pairs={{0,3},{1,2},{2,1},{3,0},{4,7},{5,6},{6,5},{7,4},{8,11},{9,10},{10,... | collective-permute-start | bytes 12296 | tf_op jit(solution)/shard_map/ppermute | solution.py:374
  22.0 3.7 %collective-permute-start.3 = (f32[1,8,128]{2,1,0:T(8,128)S(1)}, f32[1,8,128]{2,1,0:T(8,128)S(1)}, u32[]{:S(2)}, u32[]{:S(2)}) collective-permute-start(f32[1,8,128]{2,1,0:T(8,128)S(1)} %get-tuple-element.26), channel_id=1, source_target_pairs={{0,2},{1,3},{2,0},{3,1},{4,6},{5,7},{6,4},{7,5},{8,10},{9,11},{10,... | collective-permute-start | bytes 12296 | tf_op jit(solution)/shard_map/ppermute | solution.py:374
  23.2 2.5 %collective-permute-start.2 = (f32[1,8,128]{2,1,0:T(8,128)S(1)}, f32[1,8,128]{2,1,0:T(8,128)S(1)}, u32[]{:S(2)}, u32[]{:S(2)}) collective-permute-start(f32[1,8,128]{2,1,0:T(8,128)S(1)} %get-tuple-element.26), channel_id=1, source_target_pairs={{0,1},{1,0},{2,3},{3,2},{4,5},{5,4},{6,7},{7,6},{8,9},{9,8},{10,11... | collective-permute-start | bytes 12296 | tf_op jit(solution)/shard_map/ppermute | solution.py:374
  25.7 6.1 %collective-permute-start.7 = (f32[1,8,128]{2,1,0:T(8,128)S(1)}, f32[1,8,128]{2,1,0:T(8,128)S(1)}, u32[]{:S(2)}, u32[]{:S(2)}) collective-permute-start(f32[1,8,128]{2,1,0:T(8,128)S(1)} %add_add_fusion.1), channel_id=1, source_target_pairs={{0,12},{1,13},{2,14},{3,15},{4,8},{5,9},{6,10},{7,11},{8,4},{9,5},... | collective-permute-start | bytes 12296 | tf_op jit(solution)/shard_map/ppermute | solution.py:374
  26.6 5.1 %collective-permute-start.6 = (f32[1,8,128]{2,1,0:T(8,128)S(1)}, f32[1,8,128]{2,1,0:T(8,128)S(1)}, u32[]{:S(2)}, u32[]{:S(2)}) collective-permute-start(f32[1,8,128]{2,1,0:T(8,128)S(1)} %add_add_fusion.1), channel_id=1, source_target_pairs={{0,8},{1,9},{2,10},{3,11},{4,12},{5,13},{6,14},{7,15},{8,0},{9,1},... | collective-permute-start | bytes 12296 | tf_op jit(solution)/shard_map/ppermute | solution.py:374
  27.6 4.1 %collective-permute-start.5 = (f32[1,8,128]{2,1,0:T(8,128)S(1)}, f32[1,8,128]{2,1,0:T(8,128)S(1)}, u32[]{:S(2)}, u32[]{:S(2)}) collective-permute-start(f32[1,8,128]{2,1,0:T(8,128)S(1)} %add_add_fusion.1), channel_id=1, source_target_pairs={{0,4},{1,5},{2,6},{3,7},{4,0},{5,1},{6,2},{7,3},{8,12},{9,13},{10,... | collective-permute-start | bytes 12296 | tf_op jit(solution)/shard_map/ppermute | solution.py:374
